TPU v7x, 512 devices: a whole 4x8x8 slice. The times are simulated.
512 devices in a mesh: grp: 32 (over y, z_hi), chan: 16 (over z_lo, x, core).
Axes of the slice: x: 4, y: 8, z: 8 (z_hi: 4, z_lo: 2; z = z_hi * 2 + z_lo), core: 2. Of those that a mesh axis runs over, the one named last changes fastest.
Arguments:
- grad_out: bfloat16 [256, 32, 16, 128], P('grp', 'chan'), may hold values from -6 to 6
- feat_full: bfloat16 [256, 32, 16, 128], P('grp', 'chan'), may hold values from -6 to 6
- filters_full: bfloat16 [3, 3, 3, 128, 128], replicated, may hold values from -0.109375 to 0.109375
- upsample_weight: bfloat16 [2, 2, 2, 512, 128], replicated, may hold values from -0.1875 to 0.1875
- filters_half: bfloat16 [3, 3, 3, 512, 512], P(None, None, None, None, 'chan'), may hold values from -0.0546875 to 0.0546875
Outputs:
- grad_half: bfloat16 [16, 128, 8, 512], P('chan', 'grp')
- taps_grad: float32 [3, 3, 3, 128, 128], P(None, None, None, 'grp', 'chan')
All inputs are finite; a program needn't handle non-finite values.
Results may differ from a plain program's by a relative error of at most 0.0058.
Values may be sent and summed in bfloat16 or wider, within the bound.
A program may use at most 64 MiB of HBM per device.

v0:
```python
import jax
import jax.numpy as jnp
from jax import lax
from jax.sharding import PartitionSpec as P


def padded_2(cells, sides, width):
    for axis, dim in sides:
        count = lax.axis_size(axis)
        ends = count - 1
        head = lax.slice_in_dim(cells, 0, width, axis=dim)
        tail = lax.slice_in_dim(cells, cells.shape[dim] - width, cells.shape[dim], axis=dim)
        cells = jnp.concatenate(
            [
                lax.ppermute(tail, axis, [(i, (i + 1) % count) for i in range(ends)]),
                cells,
                lax.ppermute(head, axis, [((i + 1) % count, i) for i in range(ends)]),
            ],
            axis=dim,
        )
    return cells


def cut_along(value, dim, peers):
    shape = value.shape
    blocks = value.reshape(*shape[:dim], peers, shape[dim] // peers, *shape[dim + 1 :])
    return jnp.moveaxis(blocks, dim, 0)


def sent_and_summed(value, axis, dim):
    blocks = cut_along(value, dim, lax.axis_size(axis))
    arrived = lax.all_to_all(blocks, axis, split_axis=0, concat_axis=0, tiled=True)
    return arrived.sum(axis=0)


def spread_taps(padded, weight, extent, summed, swapped):
    for p in range(3):
        for q in range(3):
            for r in range(3):
                window = padded[
                    2 - p : 2 - p + extent[0], 2 - q : 2 - q + extent[1], 2 - r : 2 - r + extent[2]
                ]
                kernel = weight[q, p, r] if swapped else weight[p, q, r]
                summed = summed + jnp.einsum(
                    "xyzo,io->xyzi", window, kernel, preferred_element_type=jnp.float32
                )
    return summed


def body(grad_out, feat_full, filters_full, upsample_weight, filters_half):
    extent = grad_out.shape[:3]
    channels = grad_out.shape[3]
    stacked = jnp.stack([grad_out, feat_full])
    bordered = padded_2(stacked, (("grp", 1), ("chan", 2)), 1)
    bordered = jnp.pad(bordered, ((0, 0), (0, 0), (0, 0), (1, 1), (0, 0)))
    zeroed = jnp.zeros(extent + (channels,), jnp.float32)
    input_grad = spread_taps(bordered[0], filters_full, extent, zeroed, False).astype(jnp.bfloat16)
    features = bordered[1]
    tap_list = []
    for p in range(3):
        for q in range(3):
            for r in range(3):
                window = features[p : p + extent[0], q : q + extent[1], r : r + extent[2]]
                tap_list.append(
                    jnp.einsum(
                        "xyzi,xyzo->io", window, grad_out, preferred_element_type=jnp.float32
                    )
                )
    partial_taps = jnp.stack(tap_list).reshape(3, 3, 3, channels, channels)
    inside = sent_and_summed(partial_taps, "chan", 4)
    taps_grad = sent_and_summed(inside, "grp", 3)
    halves = input_grad.reshape(extent[0] // 2, 2, extent[1] // 2, 2, extent[2] // 2, 2, channels)
    coarse = jnp.einsum(
        "iajbkcd,abced->jike", halves, upsample_weight, preferred_element_type=jnp.float32
    ).astype(jnp.bfloat16)
    coarse_extent = coarse.shape[:3]
    wide = filters_half.shape[3]
    slab = lax.all_to_all(coarse, "chan", split_axis=3, concat_axis=0, tiled=True)
    slab = padded_2(slab, (("grp", 1),), 1)
    slab = jnp.pad(slab, ((1, 1), (0, 0), (1, 1), (0, 0)))
    count = coarse_extent[0] * lax.axis_size("chan")
    blank = jnp.zeros((count, coarse_extent[1], coarse_extent[2], wide), jnp.float32)
    result = sent_and_summed(
        spread_taps(slab, filters_half, (count, coarse_extent[1], coarse_extent[2]), blank, True),
        "chan",
        0,
    )
    grad_half = result.astype(jnp.bfloat16)
    return (grad_half, taps_grad)


def solution(mesh):
    in_specs = (
        P("grp", "chan", None, None),
        P("grp", "chan", None, None),
        P(),
        P(),
        P(None, None, None, None, "chan"),
    )
    out_specs = (P("chan", "grp", None, None), P(None, None, None, "grp", "chan"))
    return jax.shard_map(body, mesh=mesh, in_specs=in_specs, out_specs=out_specs, check_vma=False)
```

profile of v0, /device:TPU:1, one launch (start us, length us, event | category | flops | bytes accessed | tf_op | source)
XLA Modules:
  0.0 140.1 jit_solution(4277050872499112533)
XLA Ops:
  1.5 6.6 %collective-permute-start = (bf16[2,1,2,16,128]{4,3,2,1,0:T(8,128)(2,1)S(1)}, bf16[2,1,2,16,128]{4,3,2,1,0:T(8,128)(2,1)S(1)}, u32[]{:S(2)}, u32[]{:S(2)}) collective-permute-start(bf16[2,1,2,16,128]{4,3,2,1,0:T(8,128)(2,1)S(1)} %get-tuple-element.8), channel_id=1, source_target_pairs={{0,16},{16,32},{32,48},{48,64},{64,80},{80,96},{96,112},{112,128},... | collective-permute-start | bytes 49160 | tf_op jit(solution)/shard_map/ppermute | solution.py:15
  8.1 1.3 collective-permute-start.1
  9.4 6.8 %collective-permute-done.1 = bf16[2,1,2,16,128]{4,3,2,1,0:T(8,128)(2,1)S(1)} collective-permute-done((bf16[2,1,2,16,128]{4,3,2,1,0:T(8,128)(2,1)S(1)}, bf16[2,1,2,16,128]{4,3,2,1,0:T(8,128)(2,1)S(1)}, u32[]{:S(2)}, u32[]{:S(2)}) %collective-permute-start.1) | collective-permute-done | bytes 16416 | tf_op jit(solution)/shard_map/ppermute | solution.py:17
  17.2 4.8 %collective-permute-start.2 = (bf16[2,10,1,16,128]{4,3,2,1,0:T(8,128)(2,1)S(1)}, bf16[2,10,1,16,128]{4,3,2,1,0:T(8,128)(2,1)S(1)}, u32[]{:S(2)}, u32[]{:S(2)}) collective-permute-start(bf16[2,10,1,16,128]{4,3,2,1,0:T(8,128)(2,1)S(1)} %get-tuple-element.4), channel_id=1, source_target_pairs={{0,1},{1,2},{2,3},{3,4},{4,5},{5,6},{6,7},{7,8},{8,9},{9,10},{10,1... | collective-permute-start | bytes 245768 | tf_op jit(solution)/shard_map/ppermute | solution.py:15
  22.0 1.9 %collective-permute-start.3 = (bf16[2,10,1,16,128]{4,3,2,1,0:T(8,128)(2,1)S(1)}, bf16[2,10,1,16,128]{4,3,2,1,0:T(8,128)(2,1)S(1)}, u32[]{:S(2)}, u32[]{:S(2)}) collective-permute-start(bf16[2,10,1,16,128]{4,3,2,1,0:T(8,128)(2,1)S(1)} %get-tuple-element.5), channel_id=1, source_target_pairs={{1,0},{2,1},{3,2},{4,3},{5,4},{6,5},{7,6},{8,7},{9,8},{10,9},{11,1... | collective-permute-start | bytes 245768 | tf_op jit(solution)/shard_map/ppermute | solution.py:17
  24.0 3.8 %collective-permute-done.3 = bf16[2,10,1,16,128]{4,3,2,1,0:T(8,128)(2,1)S(1)} collective-permute-done((bf16[2,10,1,16,128]{4,3,2,1,0:T(8,128)(2,1)S(1)}, bf16[2,10,1,16,128]{4,3,2,1,0:T(8,128)(2,1)S(1)}, u32[]{:S(2)}, u32[]{:S(2)}) %collective-permute-start.3) | collective-permute-done | bytes 81952 | tf_op jit(solution)/shard_map/ppermute | solution.py:17
  27.8 1.1 select_maximum_fusion
  39.8 1.2 reshape.113
  41.0 6.2 %all-to-all-start = ((bf16[16,2,512]{2,1,0:T(2,128)(2,1)}), bf16[16,2,512]{2,1,0:T(2,128)(2,1)S(1)}, u32[]{:S(2)}, u32[]{:S(2)}) async-start(bf16[16,2,512]{2,1,0:T(2,128)(2,1)} %reshape.113), calls=%async_computation | async-start | bytes 65536 | tf_op jit(solution)/shard_map/all_to_all | solution.py:78
  48.0 5.0 %all-to-all-done = bf16[16,2,512]{2,1,0:T(2,128)(2,1)S(1)} async-done(((bf16[16,2,512]{2,1,0:T(2,128)(2,1)}), bf16[16,2,512]{2,1,0:T(2,128)(2,1)S(1)}, u32[]{:S(2)}, u32[]{:S(2)}) %all-to-all-start) | async-done | bytes 32800 | tf_op jit(solution)/shard_map/all_to_all | solution.py:78
  53.9 5.7 %collective-permute-start.4 = (bf16[16,1,8,32]{3,2,1,0:T(8,128)(2,1)S(1)}, bf16[16,1,8,32]{3,2,1,0:T(8,128)(2,1)S(1)}, u32[]{:S(2)}, u32[]{:S(2)}) collective-permute-start(bf16[16,1,8,32]{3,2,1,0:T(8,128)(2,1)S(1)} %get-tuple-element.6), channel_id=1, source_target_pairs={{0,16},{16,32},{32,48},{48,64},{64,80},{80,96},{96,112},{112,128},... | collective-permute-start | bytes 24584 | tf_op jit(solution)/shard_map/ppermute | solution.py:15
  59.6 1.3 collective-permute-start.5
  61.8 2.8 %copy.112 = f32[3,3,3,128,16,8]{3,5,2,1,0,4:T(8,128)} copy(f32[3,3,3,128,16,8]{3,5,4,2,1,0:T(8,128)} %bitcast.677) | data formatting | bytes 3538944 | tf_op jit(solution)/shard_map/reshape;reshape | solution.py:26
  64.6 4.2 %all-to-all-start.2 = ((f32[16,3,3,3,128,8]{4,5,3,2,1,0:T(8,128)}), f32[16,3,3,3,128,8]{4,5,3,2,1,0:T(8,128)S(1)}, u32[]{:S(2)}, u32[]{:S(2)}) async-start(f32[16,3,3,3,128,8]{4,5,3,2,1,0:T(8,128)} %bitcast.666), calls=%async_computation.2 | async-start | bytes 3538944 | tf_op jit(solution)/shard_map/all_to_all | solution.py:32
  69.0 1.1 fusion.83
  77.2 1.2 fusion
  78.5 14.2 %all-to-all-done.2 = f32[16,3,3,3,128,8]{4,5,3,2,1,0:T(8,128)S(1)} async-done(((f32[16,3,3,3,128,8]{4,5,3,2,1,0:T(8,128)}), f32[16,3,3,3,128,8]{4,5,3,2,1,0:T(8,128)S(1)}, u32[]{:S(2)}, u32[]{:S(2)}) %all-to-all-start.2) | async-done | bytes 1769504 | tf_op jit(solution)/shard_map/all_to_all | solution.py:32
  92.6 5.0 %all-to-all-start.1 = ((f32[16,1,4,8,512]{4,3,2,1,0:T(8,128)}), f32[16,1,4,8,512]{4,3,2,1,0:T(8,128)}, u32[]{:S(2)}, u32[]{:S(2)}) async-start(f32[16,1,4,8,512]{4,3,2,1,0:T(8,128)} %fusion), calls=%async_computation.1 | async-start | bytes 2097152 | tf_op jit(solution)/shard_map/all_to_all | solution.py:32
  98.3 1.5 %copy.23 = f32[32,3,3,3,4,8]{5,4,3,2,1,0:T(4,128)} copy(f32[32,3,3,3,4,8]{5,4,0,3,2,1:T(4,128)S(1)} %bitcast.670) | data formatting | bytes 221184 | tf_op jit(solution)/shard_map/transpose | solution.py:27
  99.8 3.5 %reshape.115 = f32[32,1,864]{2,1,0:T(1,128)} reshape(f32[32,3,3,3,4,8]{5,4,3,2,1,0:T(4,128)} %copy.23) | data formatting | bytes 221184
  103.3 10.2 %all-to-all-done.1 = f32[16,1,4,8,512]{4,3,2,1,0:T(8,128)} async-done(((f32[16,1,4,8,512]{4,3,2,1,0:T(8,128)}), f32[16,1,4,8,512]{4,3,2,1,0:T(8,128)}, u32[]{:S(2)}, u32[]{:S(2)}) %all-to-all-start.1) | async-done | bytes 1048608 | tf_op jit(solution)/shard_map/all_to_all | solution.py:32
  113.5 12.0 %all-to-all-start.3 = ((f32[32,1,864]{2,1,0:T(1,128)}), f32[32,1,864]{2,1,0:T(1,128)S(1)}, u32[]{:S(2)}, u32[]{:S(2)}) async-start(f32[32,1,864]{2,1,0:T(1,128)} %reshape.115), calls=%async_computation.3 | async-start | bytes 229376 | tf_op jit(solution)/shard_map/all_to_all | solution.py:32
  125.5 1.9 %reduce_sum.27 = bf16[4,8,512]{2,1,0:T(8,128)(2,1)} reduce(f32[16,1,4,8,512]{4,3,2,1,0:T(8,128)} %all-to-all-done.1, f32[]{:T(128)} %constant.4.clone.1), dimensions={0,1}, to_apply=%region_0.1 | reduce | flops 245760 | bytes 1081348 | tf_op jit(solution)/shard_map/reduce_sum | solution.py:33
  127.5 9.4 %all-to-all-done.3 = f32[32,1,864]{2,1,0:T(1,128)S(1)} async-done(((f32[32,1,864]{2,1,0:T(1,128)}), f32[32,1,864]{2,1,0:T(1,128)S(1)}, u32[]{:S(2)}, u32[]{:S(2)}) %all-to-all-start.3) | async-done | bytes 110624 | tf_op jit(solution)/shard_map/all_to_all | solution.py:32
  (109 shorter events, 25.9 us)
Async XLA Ops:
  0.6 38.5 %copy-start = (bf16[2,2,2,512,128]{4,3,2,1,0:T(8,128)(2,1)S(1)}, bf16[2,2,2,512,128]{4,3,2,1,0:T(8,128)(2,1)}, u32[]{:S(2)}) copy-start(bf16[2,2,2,512,128]{4,3,2,1,0:T(8,128)(2,1)} %param.8) | copy-start | bytes 3145732
  0.6 28.3 %copy-start.1 = (bf16[8,2,16,128]{3,2,1,0:T(8,128)(2,1)S(1)}, bf16[8,2,16,128]{3,2,1,0:T(8,128)(2,1)}, u32[]{:S(2)}) copy-start(bf16[8,2,16,128]{3,2,1,0:T(8,128)(2,1)} %param.5) | copy-start | bytes 196612
  1.5 7.9 %collective-permute-start = (bf16[2,1,2,16,128]{4,3,2,1,0:T(8,128)(2,1)S(1)}, bf16[2,1,2,16,128]{4,3,2,1,0:T(8,128)(2,1)S(1)}, u32[]{:S(2)}, u32[]{:S(2)}) collective-permute-start(bf16[2,1,2,16,128]{4,3,2,1,0:T(8,128)(2,1)S(1)} %get-tuple-element.8), channel_id=1, source_target_pairs={{0,16},{16,32},{32,48},{48,64},{64,80},{80,96},{96,112},{112,128},... | collective-permute-start | bytes 49160 | tf_op jit(solution)/shard_map/ppermute | solution.py:15
  8.1 8.1 %collective-permute-start.1 = (bf16[2,1,2,16,128]{4,3,2,1,0:T(8,128)(2,1)S(1)}, bf16[2,1,2,16,128]{4,3,2,1,0:T(8,128)(2,1)S(1)}, u32[]{:S(2)}, u32[]{:S(2)}) collective-permute-start(bf16[2,1,2,16,128]{4,3,2,1,0:T(8,128)(2,1)S(1)} %get-tuple-element.9), channel_id=1, source_target_pairs={{16,0},{32,16},{48,32},{64,48},{80,64},{96,80},{112,96},{128,112},... | collective-permute-start | bytes 49160 | tf_op jit(solution)/shard_map/ppermute | solution.py:17
  17.2 6.8 %collective-permute-start.2 = (bf16[2,10,1,16,128]{4,3,2,1,0:T(8,128)(2,1)S(1)}, bf16[2,10,1,16,128]{4,3,2,1,0:T(8,128)(2,1)S(1)}, u32[]{:S(2)}, u32[]{:S(2)}) collective-permute-start(bf16[2,10,1,16,128]{4,3,2,1,0:T(8,128)(2,1)S(1)} %get-tuple-element.4), channel_id=1, source_target_pairs={{0,1},{1,2},{2,3},{3,4},{4,5},{5,6},{6,7},{7,8},{8,9},{9,10},{10,1... | collective-permute-start | bytes 245768 | tf_op jit(solution)/shard_map/ppermute | solution.py:15
  22.0 5.8 %collective-permute-start.3 = (bf16[2,10,1,16,128]{4,3,2,1,0:T(8,128)(2,1)S(1)}, bf16[2,10,1,16,128]{4,3,2,1,0:T(8,128)(2,1)S(1)}, u32[]{:S(2)}, u32[]{:S(2)}) collective-permute-start(bf16[2,10,1,16,128]{4,3,2,1,0:T(8,128)(2,1)S(1)} %get-tuple-element.5), channel_id=1, source_target_pairs={{1,0},{2,1},{3,2},{4,3},{5,4},{6,5},{7,6},{8,7},{9,8},{10,9},{11,1... | collective-permute-start | bytes 245768 | tf_op jit(solution)/shard_map/ppermute | solution.py:17
  30.8 3.8 %copy-start.4 = (bf16[3,3,3,128,128]{4,3,2,1,0:T(8,128)(2,1)S(1)}, bf16[3,3,3,128,128]{4,3,2,1,0:T(8,128)(2,1)}, u32[]{:S(2)}) copy-start(bf16[3,3,3,128,128]{4,3,2,1,0:T(8,128)(2,1)} %param.7) | copy-start | bytes 2654212
  34.5 1.9 %copy-start.2 = (f32[27,128,128]{1,2,0:T(8,128)}, f32[27,128,128]{1,2,0:T(8,128)S(1)}, u32[]{:S(2)}) copy-start(f32[27,128,128]{1,2,0:T(8,128)S(1)} %fusion.8) | copy-start | bytes 5308420
  41.0 12.0 %all-to-all-start = ((bf16[16,2,512]{2,1,0:T(2,128)(2,1)}), bf16[16,2,512]{2,1,0:T(2,128)(2,1)S(1)}, u32[]{:S(2)}, u32[]{:S(2)}) async-start(bf16[16,2,512]{2,1,0:T(2,128)(2,1)} %reshape.113), calls=%async_computation | async-start | bytes 65536 | tf_op jit(solution)/shard_map/all_to_all | solution.py:78
  53.9 14.9 %collective-permute-start.4 = (bf16[16,1,8,32]{3,2,1,0:T(8,128)(2,1)S(1)}, bf16[16,1,8,32]{3,2,1,0:T(8,128)(2,1)S(1)}, u32[]{:S(2)}, u32[]{:S(2)}) collective-permute-start(bf16[16,1,8,32]{3,2,1,0:T(8,128)(2,1)S(1)} %get-tuple-element.6), channel_id=1, source_target_pairs={{0,16},{16,32},{32,48},{48,64},{64,80},{80,96},{96,112},{112,128},... | collective-permute-start | bytes 24584 | tf_op jit(solution)/shard_map/ppermute | solution.py:15
  59.6 9.1 %collective-permute-start.5 = (bf16[16,1,8,32]{3,2,1,0:T(8,128)(2,1)S(1)}, bf16[16,1,8,32]{3,2,1,0:T(8,128)(2,1)S(1)}, u32[]{:S(2)}, u32[]{:S(2)}) collective-permute-start(bf16[16,1,8,32]{3,2,1,0:T(8,128)(2,1)S(1)} %get-tuple-element.7), channel_id=1, source_target_pairs={{16,0},{32,16},{48,32},{64,48},{80,64},{96,80},{112,96},{128,112},... | collective-permute-start | bytes 24584 | tf_op jit(solution)/shard_map/ppermute | solution.py:17
  64.6 28.0 %all-to-all-start.2 = ((f32[16,3,3,3,128,8]{4,5,3,2,1,0:T(8,128)}), f32[16,3,3,3,128,8]{4,5,3,2,1,0:T(8,128)S(1)}, u32[]{:S(2)}, u32[]{:S(2)}) async-start(f32[16,3,3,3,128,8]{4,5,3,2,1,0:T(8,128)} %bitcast.666), calls=%async_computation.2 | async-start | bytes 3538944 | tf_op jit(solution)/shard_map/all_to_all | solution.py:32
  68.8 1.3 copy-start.3
  92.6 20.9 %all-to-all-start.1 = ((f32[16,1,4,8,512]{4,3,2,1,0:T(8,128)}), f32[16,1,4,8,512]{4,3,2,1,0:T(8,128)}, u32[]{:S(2)}, u32[]{:S(2)}) async-start(f32[16,1,4,8,512]{4,3,2,1,0:T(8,128)} %fusion), calls=%async_computation.1 | async-start | bytes 2097152 | tf_op jit(solution)/shard_map/all_to_all | solution.py:32
  113.5 23.3 %all-to-all-start.3 = ((f32[32,1,864]{2,1,0:T(1,128)}), f32[32,1,864]{2,1,0:T(1,128)S(1)}, u32[]{:S(2)}, u32[]{:S(2)}) async-start(f32[32,1,864]{2,1,0:T(1,128)} %reshape.115), calls=%async_computation.3 | async-start | bytes 229376 | tf_op jit(solution)/shard_map/all_to_all | solution.py:32
where the time goes:
time: 141 us; the launch traced here: 140 us
  waiting for transfers between devices  49.4 us (35%)
  starting transfers between devices  49.1 us (35%)
  matrix products  21.1 us (15%)
  local copies, waits for them, and re-layouts  12.2 us (9%)
  other arithmetic  6.97 us (5%)
    all_to_all x3, waiting for transfers between devices, sent_and_summed(): lax.all_to_all(blocks, axis, split_axis=0, concat_axis=0, tiled=True)  33.7 us
    all_to_all x3, starting transfers between devices, sent_and_summed(): lax.all_to_all(blocks, axis, split_axis=0, concat_axis=0, tiled=True)  21.2 us
    ppermute x3, starting transfers between devices, padded_2(): lax.ppermute(tail, axis, [(i, (i + 1) % count) for i in range(ends)])  17.2 us
    dot_general x54, matrix products, spread_taps(): jnp.einsum('xyzo,io->xyzi', window, kernel, preferred_element_type=jnp.fl...  13.7 us
    ppermute x3, waiting for transfers between devices, padded_2(): lax.ppermute(head, axis, [((i + 1) % count, i) for i in range(ends)])  10.7 us
    dot_general x27, matrix products, body(): jnp.einsum('xyzi,xyzo->io', window, grad_out, preferred_element_type=jnp....  7.02 us
    unnamed x14, local copies, waits for them, and re-layouts  6.18 us
    all_to_all x1, starting transfers between devices, body(): lax.all_to_all(coarse, 'chan', split_axis=3, concat_axis=0, tiled=True)  6.17 us
  transfers between devices with their start and end apart: 10, of which 6 were waited for; matrix products, arithmetic and copies ran while one was open for 15% of the time, Pallas kernels for 0%

commit v1 on v0

v1 whole, which is shorter than its diff:
```python
import jax
import jax.numpy as jnp
from jax import lax
from jax.experimental import pallas as pl
from jax.experimental.pallas import tpu as pltpu
from jax.sharding import PartitionSpec as P

F32 = jnp.float32
BF16 = jnp.bfloat16
MESH = pl.DeviceIdType.MESH
NT = (((1,), (1,)), ((), ()))
TN = (((0,), (0,)), ((), ()))
ZHI = 4


def kernel(
    go, fe, wf, uw, wh,
    gh_out, tg_out,
    G, FE, WF, UP, WP, IG,
    T, XS, XR, SS, SR,
    PS, PR, SA, FS, FR,
    VT, YS, YR, ZS, ZR,
    lsem, hs, hr, ws, wr, xs, xr, ss, sr, ps, pr, fs, fr, ys, yr, zs, zr,
):
    g = lax.axis_index("grp")
    c = lax.axis_index("chan")
    ngrp = lax.axis_size("grp")
    nchan = lax.axis_size("chan")
    nchip = nchan // 2
    ny = ngrp // ZHI
    y, zh = g // ZHI, lax.rem(g, ZHI)
    chip, core = c // 2, lax.rem(c, 2)

    def dev(gi, ci):
        return {"grp": gi, "chan": ci}

    def remote(src, dst, send, recv, gi, ci):
        return pltpu.make_async_remote_copy(
            src_ref=src, dst_ref=dst, send_sem=send, recv_sem=recv,
            device_id=dev(gi, ci), device_id_type=MESH,
        )

    def group_of(s):
        return lax.rem(c + s, nchan)

    def ygrp(s):
        return lax.rem(y + s, ny) * ZHI + zh

    def zgrp(s):
        return y * ZHI + lax.rem(zh + s, ZHI)

    l_go = pltpu.make_async_copy(go, G.at[3:11, 1:3], lsem.at[0])
    l_wh = [
        pltpu.make_async_copy(
            wh.at[t], WP.at[:, :, pl.ds(pl.multiple_of(t * 64 + core * 32, 32), 32), :], lsem.at[1 + t]
        )
        for t in range(3)
    ]
    l_fe = pltpu.make_async_copy(fe, FE, lsem.at[4])
    l_wf = pltpu.make_async_copy(wf, WF, lsem.at[5])
    l_up = pltpu.make_async_copy(uw, UP, lsem.at[6])
    l_go.start()
    l_fe.start()
    for t in range(3):
        l_wh[t].start()
    l_wf.start()
    l_up.start()

    barrier = pltpu.get_barrier_semaphore()

    def hello(gi, ci):
        pl.semaphore_signal(barrier, inc=1, device_id=dev(gi, ci), device_id_type=MESH)

    def hello_group(s, _):
        hello(g, group_of(s))
        return 0

    def hello_y(s, _):
        hello(ygrp(s), c)
        return 0

    def hello_z(s, _):
        hello(zgrp(s), c)
        return 0

    for dg in (1, ngrp - 1):
        for dc in (0, 1, nchan - 1):
            hello(lax.rem(g + dg, ngrp), group_of(dc))
    lax.fori_loop(1, nchan, hello_group, 0)
    lax.fori_loop(1, ny, hello_y, 0)
    lax.fori_loop(1, ZHI, hello_z, 0)

    PR[0] = jnp.zeros(PR.shape[1:], BF16)
    PR[nchan + 1] = jnp.zeros(PR.shape[1:], BF16)
    WP[:, :, 192:256, :] = jnp.zeros((3, 3, 64, WP.shape[3]), BF16)
    T[:, :, 216:224, :] = jnp.zeros((2, nchip, 8, 128), F32)
    l_fe.wait()
    feat = FE[...].reshape(256, 128).astype(F32)
    z_of = lax.broadcasted_iota(jnp.int32, (256, 128), 0) % 16
    before = jnp.where(z_of > 0, pltpu.roll(feat, 1, 0), 0.0)
    after = jnp.where(z_of < 15, pltpu.roll(feat, 255, 0), 0.0)
    feat3 = jnp.concatenate([before, feat, after], axis=1).astype(BF16)
    l_go.wait()

    pl.semaphore_wait(barrier, (nchan - 1) + (ny - 1) + (ZHI - 1) + 6)

    xsrc = {0: (3, 11), 1: (8, 11), 2: (3, 6)}
    xdst = {0: (3, 11), 1: (0, 3), 2: (11, 14)}
    ysrc = {0: (1, 3), 1: (2, 3), 2: (1, 2)}
    ydst = {0: (1, 3), 1: (0, 1), 2: (3, 4)}
    gstep = {0: 0, 1: 1, 2: ngrp - 1}
    cstep = {0: 0, 1: 1, 2: nchan - 1}
    halos = []
    for a, b in ((1, 0), (2, 0), (1, 1), (1, 2), (2, 1), (2, 2), (0, 1), (0, 2)):
        halos.append(
            remote(
                G.at[xsrc[a][0]:xsrc[a][1], ysrc[b][0]:ysrc[b][1]],
                G.at[xdst[a][0]:xdst[a][1], ydst[b][0]:ydst[b][1]],
                hs.at[a * 3 + b], hr.at[a * 3 + b],
                lax.rem(g + gstep[a], ngrp), group_of(cstep[b]),
            )
        )
    for h in halos:
        h.start()
    other = c + 1 - 2 * core
    wcopies = []
    for t in range(3):
        l_wh[t].wait()
        rows = WP.at[:, :, pl.ds(pl.multiple_of(t * 64 + core * 32, 32), 32), :]
        wcopies.append(remote(rows, rows, ws.at[t], wr.at[t], g, other))
        wcopies[-1].start()
    l_wf.wait()
    l_up.wait()
    for h in halos:
        h.wait_recv()

    @pl.when(g == 0)
    def _():
        G[0:3] = jnp.zeros((3,) + G.shape[1:], BF16)

    @pl.when(g == ngrp - 1)
    def _():
        G[11:14] = jnp.zeros((3,) + G.shape[1:], BF16)

    @pl.when(c == 0)
    def _():
        G[:, 0:1] = jnp.zeros((14, 1, 16, 128), BF16)

    @pl.when(c == nchan - 1)
    def _():
        G[:, 3:4] = jnp.zeros((14, 1, 16, 128), BF16)

    for tx in range(3):
        window = jnp.concatenate(
            [G[4 - tx:12 - tx, 2 - ty:4 - ty].reshape(256, 128) for ty in range(3)], axis=1
        )
        part = lax.dot_general(window, feat3, TN, preferred_element_type=F32)
        for ty in range(3):
            rows = part[ty * 128:(ty + 1) * 128].reshape(nchip, 2, 8, 384)
            for tz in range(3):
                at = ((tx * 3 + ty) * 3 + tz) * 8
                for k in range(2):
                    T[k, :, at:at + 8, :] = rows[:, k, :, tz * 128:(tz + 1) * 128]
    XS[...] = T[1 - core].astype(BF16)
    xcopy = remote(XS, XR, xs, xr, g, other)
    xcopy.start()

    lhs = jnp.concatenate(
        [
            G[2 - tx:14 - tx, 2 - ty:4 - ty].reshape(384, 128)
            for tx in range(3)
            for ty in range(3)
        ],
        axis=1,
    )
    rhs = jnp.concatenate(
        [WF[tx, ty].reshape(384, 128) for tx in range(3) for ty in range(3)], axis=1
    )
    grown = lax.dot_general(lhs, rhs, NT, preferred_element_type=F32)
    z_at = lax.broadcasted_iota(jnp.int32, (384, 128), 0) % 16
    up = jnp.where(z_at < 15, pltpu.roll(grown[:, 0:128], 383, 0), 0.0)
    down = jnp.where(z_at > 0, pltpu.roll(grown[:, 256:384], 1, 0), 0.0)
    IG[...] = grown[:, 128:256] + up + down

    coarse = jnp.zeros((48, 512), F32)
    for a in range(2):
        for b in range(2):
            cells = jnp.concatenate(
                [
                    jnp.concatenate(
                        [IG[pl.ds(((2 * i + a) * 2 + b) * 16 + k, 8, stride=2), :] for i in range(6)],
                        axis=0,
                    )
                    for k in range(2)
                ],
                axis=1,
            ).astype(BF16)
            weight = jnp.concatenate([UP[a, b, 0], UP[a, b, 1]], axis=1)
            coarse = coarse + lax.dot_general(cells, weight, NT, preferred_element_type=F32)
    row_of = lax.broadcasted_iota(jnp.int32, (48, 512), 0)
    outside = ((row_of < 8) & (g == 0)) | ((row_of >= 40) & (g == ngrp - 1))
    coarse = jnp.where(outside, 0.0, coarse)
    low = lax.broadcasted_iota(jnp.int32, (8, 128), 1) < 64
    for q in range(4):
        block = coarse[:, q * 128:(q + 1) * 128]
        turned = pltpu.roll(block, 64, 1)
        for half in range(2):
            same, swap = (block, turned) if half == 0 else (turned, block)
            d = 2 * q + half
            for k in range(2):
                pair = []
                for i in (2 * k, 2 * k + 1):
                    s0, s1, s2 = (i + 2) * 8, (i + 1) * 8, i * 8
                    first = jnp.where(low, same[s0:s0 + 8], swap[s1:s1 + 8])
                    pair.append(jnp.concatenate([first, same[s2:s2 + 8]], axis=1))
                PS[2 * d + k] = jnp.concatenate(pair, axis=0).astype(BF16)

    def pcopy(s):
        d = group_of(s)
        return remote(PS.at[d], PR.at[c + 1], ps.at[d], pr.at[c], g, d)

    def psend(s, _):
        pcopy(s).start()
        return 0

    lax.fori_loop(1, nchan, psend, 0)
    PR[c + 1] = PS[c]

    xcopy.wait_recv()
    T[core] = T[core] + XR[...].astype(F32)
    SS[...] = T[core].astype(BF16)

    def scopy(s):
        d = lax.rem(chip + s, nchip)
        return remote(SS.at[d], SR.at[chip], ss.at[d], sr.at[chip], g, 2 * d + core)

    def ssend(s, _):
        scopy(s).start()
        return 0

    lax.fori_loop(1, nchip, ssend, 0)

    for w in wcopies:
        w.wait_recv()

    def precv(s, _):
        o = group_of(s)
        remote(PS.at[o], PR.at[o + 1], ps.at[o], pr.at[o], g, o).wait_recv()
        return 0

    lax.fori_loop(1, nchan, precv, 0)
    rows = (nchan + 2) * 16
    slab = PR[...].reshape(rows, 256).astype(F32)
    k_of = lax.broadcasted_iota(jnp.int32, (rows, 256), 0) % 8
    SA[0] = jnp.where(k_of < 7, pltpu.roll(slab, rows - 1, 0), 0.0).astype(BF16).reshape(SA.shape[1:])
    SA[1] = PR[...]
    SA[2] = jnp.where(k_of > 0, pltpu.roll(slab, 1, 0), 0.0).astype(BF16).reshape(SA.shape[1:])
    lhs = jnp.concatenate(
        [
            SA[tz, 2 - ty:2 - ty + nchan].reshape(nchan * 16, 256)
            for ty in range(3)
            for tz in range(3)
        ],
        axis=1,
    )
    part = jnp.dot(lhs, WP[...].reshape(9 * 256, 512), preferred_element_type=F32)
    FS[...] = part.astype(BF16).reshape(FS.shape)

    def fcopy(s):
        d = group_of(s)
        return remote(FS.at[d], FR.at[c], fs.at[d], fr.at[c], g, d)

    def fsend(s, _):
        fcopy(s).start()
        return 0

    lax.fori_loop(1, nchan, fsend, 0)
    FR[c] = FS[c]

    total = T[core, chip]

    def srecv(s, acc):
        o = lax.rem(chip + s, nchip)
        remote(SS.at[o], SR.at[o], ss.at[o], sr.at[o], g, 2 * o + core).wait_recv()
        return acc + SR[o].astype(F32)

    total = lax.fori_loop(1, nchip, srecv, total)
    flipped = jnp.concatenate([total, jnp.zeros((32, 128), F32)], axis=0).T
    VT[...] = flipped.reshape(VT.shape)
    YS[...] = flipped.astype(BF16).reshape(YS.shape)

    def ycopy(s):
        d = lax.rem(y + s, ny)
        return remote(YS.at[d], YR.at[y], ys.at[d], yr.at[y], d * ZHI + zh, c)

    def ysend(s, _):
        ycopy(s).start()
        return 0

    lax.fori_loop(1, ny, ysend, 0)

    def frecv(s, _):
        o = group_of(s)
        remote(FS.at[o], FR.at[o], fs.at[o], fr.at[o], g, o).wait_recv()
        return 0

    lax.fori_loop(1, nchan, frecv, 0)
    for k in range(2):
        acc = FR[k].astype(F32)
        for p in range(1, nchan // 2):
            acc = acc + FR[2 * p + k].astype(F32)
        gh_out[k * 16:(k + 1) * 16, :] = acc.astype(BF16)

    def yrecv(s, acc):
        o = lax.rem(y + s, ny)
        remote(YS.at[o], YR.at[o], ys.at[o], yr.at[o], o * ZHI + zh, c).wait_recv()
        return acc + YR[o].astype(F32)

    v2 = lax.fori_loop(1, ny, yrecv, VT[y])
    for q in range(ZHI):
        ZS[q] = jnp.concatenate([v2[4 * q:4 * q + 4], jnp.zeros((4, 256), F32)], axis=0)

    def zcopy(s):
        d = lax.rem(zh + s, ZHI)
        return remote(ZS.at[d], ZR.at[zh], zs.at[d], zr.at[zh], y * ZHI + d, c)

    def zsend(s, _):
        zcopy(s).start()
        return 0

    lax.fori_loop(1, ZHI, zsend, 0)

    def zrecv(s, acc):
        o = lax.rem(zh + s, ZHI)
        remote(ZS.at[o], ZR.at[o], zs.at[o], zr.at[o], y * ZHI + o, c).wait_recv()
        return acc + ZR[o]

    v3 = lax.fori_loop(1, ZHI, zrecv, ZS[zh])
    for t in range(27):
        tg_out[t] = v3[0:4, 8 * t:8 * t + 8]

    for h in halos:
        h.wait_send()
    for w in wcopies:
        w.wait_send()
    xcopy.wait_send()

    def sent_group(s, _):
        pcopy(s).wait_send()
        fcopy(s).wait_send()
        return 0

    def sent_chip(s, _):
        scopy(s).wait_send()
        return 0

    def sent_y(s, _):
        ycopy(s).wait_send()
        return 0

    def sent_z(s, _):
        zcopy(s).wait_send()
        return 0

    lax.fori_loop(1, nchan, sent_group, 0)
    lax.fori_loop(1, nchip, sent_chip, 0)
    lax.fori_loop(1, ny, sent_y, 0)
    lax.fori_loop(1, ZHI, sent_z, 0)


def body(grad_out, feat_full, filters_full, upsample_weight, filters_half):
    nchan = lax.axis_size("chan")
    ny = lax.axis_size("grp") // ZHI
    nchip = nchan // 2
    wide = filters_half.shape[3]
    turned = jnp.swapaxes(filters_half, 3, 4)
    V = pltpu.VMEM
    D = pltpu.SemaphoreType.DMA
    anyspace = pl.BlockSpec(memory_space=pl.ANY)
    vmem = pl.BlockSpec(memory_space=pltpu.VMEM)
    grad_half, taps = pl.pallas_call(
        kernel,
        out_shape=(
            jax.ShapeDtypeStruct((32, wide), BF16),
            jax.ShapeDtypeStruct((27, 4, 8), F32),
        ),
        in_specs=[anyspace] * 5,
        out_specs=(vmem, vmem),
        scratch_shapes=[
            V((14, 4, 16, 128), BF16),
            V((8, 2, 16, 128), BF16),
            V((3, 3, 3, 128, 128), BF16),
            V((2, 2, 2, wide, 128), BF16),
            V((3, 3, 256, wide), BF16),
            V((384, 128), F32),
            V((2, nchip, 224, 128), F32),
            V((nchip, 224, 128), BF16),
            V((nchip, 224, 128), BF16),
            V((nchip, 224, 128), BF16),
            V((nchip, 224, 128), BF16),
            V((nchan, 16, 256), BF16),
            V((nchan + 2, 16, 256), BF16),
            V((3, nchan + 2, 16, 256), BF16),
            V((nchan, 16, wide), BF16),
            V((nchan, 16, wide), BF16),
            V((ny, 16, 256), F32),
            V((ny, 16, 256), BF16),
            V((ny, 16, 256), BF16),
            V((ZHI, 8, 256), F32),
            V((ZHI, 8, 256), F32),
            D((7,)),
            D((9,)), D((9,)),
            D((3,)), D((3,)),
            D, D,
            D((nchip,)), D((nchip,)),
            D((nchan,)), D((nchan,)),
            D((nchan,)), D((nchan,)),
            D((ny,)), D((ny,)),
            D((ZHI,)), D((ZHI,)),
        ],
        compiler_params=pltpu.CompilerParams(collective_id=0, has_side_effects=True),
    )(grad_out, feat_full, filters_full, upsample_weight, turned)
    return grad_half.reshape(1, 4, 8, wide), taps.reshape(3, 3, 3, 4, 8)


def solution(mesh):
    in_specs = (
        P("grp", "chan", None, None),
        P("grp", "chan", None, None),
        P(),
        P(),
        P(None, None, None, None, "chan"),
    )
    out_specs = (P("chan", "grp", None, None), P(None, None, None, "grp", "chan"))
    return jax.shard_map(body, mesh=mesh, in_specs=in_specs, out_specs=out_specs, check_vma=False)
```

time: 141 us -> 46.3 us (0.33)
  the two profiles are of different devices: /device:TPU:1 before, /device:TPU:6 now
where the time goes in v1:
time: 46.3 us; the launch traced here: 46.1 us
  Pallas kernels  43.5 us (94%)
  local copies, waits for them, and re-layouts  2.02 us (4%)
  between operations  0.65 us (1%)
    pallas_call x1, Pallas kernels, body(): pl.pallas_call(kernel, out_shape=(jax.ShapeDtypeStruct((32, wide), BF16),...  43.5 us
    unnamed x4, local copies, waits for them, and re-layouts  2.02 us

profile of v1, /device:TPU:6, one launch (start us, length us, event | category | flops | bytes accessed | tf_op | source)
XLA Modules:
  0.0 46.1 jit_solution(940862563087589966)
XLA Ops:
  0.6 43.5 %shard_map.68 = (bf16[32,512]{1,0:T(8,128)(2,1)}, f32[27,4,8]{2,1,0:T(4,128)}) custom-call(bf16[8,2,16,128]{3,2,1,0:T(8,128)(2,1)} %go.1, bf16[8,2,16,128]{3,2,1,0:T(8,128)(2,1)} %fe.1, bf16[3,3,3,128,128]{4,3,2,1,0:T(8,128)(2,1)} %wf.1, bf16[2,2,2,512,128]{4,3,2,1,0:T(8,128)(2,1)} %uw.1, bf16[3,3,3,32,512]{4,3,2,1,0:T(8,128)(2,1)} %bitcast.3), custom_call_target="tpu_custom_call" | custom-call | tf_op jit(solution)/shard_map/pallas_call | solution.py:381
  44.1 0.0 copy-start
  44.1 1.4 %copy.9 = bf16[1,4,8,512]{3,2,1,0:T(8,128)(2,1)} copy(bf16[1,4,8,512]{3,2,1,0:T(8,128)(2,1)} %bitcast.5) | data formatting | bytes 65536
  45.5 0.0 copy-done
  45.5 0.6 %copy.10 = f32[3,3,3,4,8]{4,3,2,1,0:T(4,128)} copy(f32[3,3,3,4,8]{4,3,2,1,0:T(4,128)S(1)} %bitcast.4) | data formatting | bytes 6912
Async XLA Ops:
  44.1 1.4 %copy-start = (f32[27,4,8]{2,1,0:T(4,128)S(1)}, f32[27,4,8]{2,1,0:T(4,128)}, u32[]{:S(2)}) copy-start(f32[27,4,8]{2,1,0:T(4,128)} %get-tuple-element.5) | copy-start | bytes 10372

commit v2 on v1

--- a/solution.py
+++ b/solution.py
@@ -20,7 +20,7 @@
     T, XS, XR, SS, SR,
     PS, PR, SA, FS, FR,
     VT, YS, YR, ZS, ZR,
-    lsem, hs, hr, ws, wr, xs, xr, ss, sr, ps, pr, fs, fr, ys, yr, zs, zr,
+    lsem, hs, hr, hs2, hr2, ws, wr, xs, xr, ss, sr, ps, pr, fs, fr, ys, yr, zs, zr,
 ):
     g = lax.axis_index("grp")
     c = lax.axis_index("chan")
@@ -48,6 +48,12 @@
 
     def zgrp(s):
         return y * ZHI + lax.rem(zh + s, ZHI)
+
+    def ycopy(s, part):
+        d = lax.rem(y + s, ny)
+        return remote(
+            YS.at[part, d], YR.at[part, y], ys.at[part, d], yr.at[part, y], d * ZHI + zh, c
+        )
 
     l_go = pltpu.make_async_copy(go, G.at[3:11, 1:3], lsem.at[0])
     l_wh = [
@@ -84,11 +90,11 @@
         return 0
 
     for dg in (1, ngrp - 1):
-        for dc in (0, 1, nchan - 1):
+        for dc in (1, nchan - 1, 0):
             hello(lax.rem(g + dg, ngrp), group_of(dc))
-    lax.fori_loop(1, nchan, hello_group, 0)
     lax.fori_loop(1, ny, hello_y, 0)
     lax.fori_loop(1, ZHI, hello_z, 0)
+    lax.fori_loop(1, nchan, hello_group, 0)
 
     PR[0] = jnp.zeros(PR.shape[1:], BF16)
     PR[nchan + 1] = jnp.zeros(PR.shape[1:], BF16)
@@ -104,23 +110,34 @@
 
     pl.semaphore_wait(barrier, (nchan - 1) + (ny - 1) + (ZHI - 1) + 6)
 
-    xsrc = {0: (3, 11), 1: (8, 11), 2: (3, 6)}
-    xdst = {0: (3, 11), 1: (0, 3), 2: (11, 14)}
     ysrc = {0: (1, 3), 1: (2, 3), 2: (1, 2)}
     ydst = {0: (1, 3), 1: (0, 1), 2: (3, 4)}
     gstep = {0: 0, 1: 1, 2: ngrp - 1}
     cstep = {0: 0, 1: 1, 2: nchan - 1}
-    halos = []
-    for a, b in ((1, 0), (2, 0), (1, 1), (1, 2), (2, 1), (2, 2), (0, 1), (0, 2)):
-        halos.append(
-            remote(
-                G.at[xsrc[a][0]:xsrc[a][1], ysrc[b][0]:ysrc[b][1]],
-                G.at[xdst[a][0]:xdst[a][1], ydst[b][0]:ydst[b][1]],
-                hs.at[a * 3 + b], hr.at[a * 3 + b],
-                lax.rem(g + gstep[a], ngrp), group_of(cstep[b]),
-            )
-        )
-    for h in halos:
+
+    def halo(a, b, src, dst, send, recv):
+        return remote(
+            G.at[src[0]:src[1], ysrc[b][0]:ysrc[b][1]],
+            G.at[dst[0]:dst[1], ydst[b][0]:ydst[b][1]],
+            send.at[a * 3 + b], recv.at[a * 3 + b],
+            lax.rem(g + gstep[a], ngrp), group_of(cstep[b]),
+        )
+
+    near_src = {0: (3, 11), 1: (10, 11), 2: (3, 4)}
+    near_dst = {0: (3, 11), 1: (2, 3), 2: (11, 12)}
+    far_src = {1: (8, 10), 2: (4, 6)}
+    far_dst = {1: (0, 2), 2: (12, 14)}
+    near = [
+        halo(a, b, near_src[a], near_dst[a], hs, hr)
+        for a, b in ((1, 1), (1, 2), (2, 1), (2, 2), (1, 0), (2, 0), (0, 1), (0, 2))
+    ]
+    far = [
+        halo(a, b, far_src[a], far_dst[a], hs2, hr2)
+        for a, b in ((1, 1), (1, 2), (2, 1), (2, 2), (1, 0), (2, 0))
+    ]
+    for h in near:
+        h.start()
+    for h in far:
         h.start()
     other = c + 1 - 2 * core
     wcopies = []
@@ -129,27 +146,26 @@
         rows = WP.at[:, :, pl.ds(pl.multiple_of(t * 64 + core * 32, 32), 32), :]
         wcopies.append(remote(rows, rows, ws.at[t], wr.at[t], g, other))
         wcopies[-1].start()
-    l_wf.wait()
-    l_up.wait()
-    for h in halos:
+    for h in near:
         h.wait_recv()
 
     @pl.when(g == 0)
     def _():
-        G[0:3] = jnp.zeros((3,) + G.shape[1:], BF16)
+        G[2:3] = jnp.zeros((1,) + G.shape[1:], BF16)
 
     @pl.when(g == ngrp - 1)
     def _():
-        G[11:14] = jnp.zeros((3,) + G.shape[1:], BF16)
+        G[11:12] = jnp.zeros((1,) + G.shape[1:], BF16)
 
     @pl.when(c == 0)
     def _():
-        G[:, 0:1] = jnp.zeros((14, 1, 16, 128), BF16)
+        G[2:12, 0:1] = jnp.zeros((10, 1, 16, 128), BF16)
 
     @pl.when(c == nchan - 1)
     def _():
-        G[:, 3:4] = jnp.zeros((14, 1, 16, 128), BF16)
-
+        G[2:12, 3:4] = jnp.zeros((10, 1, 16, 128), BF16)
+
+    xcopies = []
     for tx in range(3):
         window = jnp.concatenate(
             [G[4 - tx:12 - tx, 2 - ty:4 - ty].reshape(256, 128) for ty in range(3)], axis=1
@@ -161,9 +177,32 @@
                 at = ((tx * 3 + ty) * 3 + tz) * 8
                 for k in range(2):
                     T[k, :, at:at + 8, :] = rows[:, k, :, tz * 128:(tz + 1) * 128]
-    XS[...] = T[1 - core].astype(BF16)
-    xcopy = remote(XS, XR, xs, xr, g, other)
-    xcopy.start()
+        part_rows = pl.ds(tx * 72, 80 if tx == 2 else 72)
+        XS[:, part_rows, :] = T[1 - core, :, part_rows, :].astype(BF16)
+        xcopies.append(remote(XS.at[:, part_rows, :], XR.at[:, part_rows, :], xs.at[tx], xr.at[tx], g, other))
+        xcopies[-1].start()
+
+    l_wf.wait()
+    for h in far:
+        h.wait_recv()
+
+    @pl.when(g == 0)
+    def _():
+        G[0:2] = jnp.zeros((2,) + G.shape[1:], BF16)
+
+    @pl.when(g == ngrp - 1)
+    def _():
+        G[12:14] = jnp.zeros((2,) + G.shape[1:], BF16)
+
+    @pl.when(c == 0)
+    def _():
+        G[0:2, 0:1] = jnp.zeros((2, 1, 16, 128), BF16)
+        G[12:14, 0:1] = jnp.zeros((2, 1, 16, 128), BF16)
+
+    @pl.when(c == nchan - 1)
+    def _():
+        G[0:2, 3:4] = jnp.zeros((2, 1, 16, 128), BF16)
+        G[12:14, 3:4] = jnp.zeros((2, 1, 16, 128), BF16)
 
     lhs = jnp.concatenate(
         [
@@ -182,6 +221,27 @@
     down = jnp.where(z_at > 0, pltpu.roll(grown[:, 256:384], 1, 0), 0.0)
     IG[...] = grown[:, 128:256] + up + down
 
+    for x in xcopies:
+        x.wait_recv()
+    T[core] = T[core] + XR[...].astype(F32)
+    SS[...] = T[core].astype(BF16)
+
+    def scopy(s, part):
+        d = lax.rem(chip + s, nchip)
+        rows = pl.ds(0, 128) if part == 0 else pl.ds(128, 96)
+        return remote(
+            SS.at[d, rows], SR.at[chip, rows], ss.at[part, d], sr.at[part, chip], g, 2 * d + core
+        )
+
+    for part in range(2):
+
+        def ssend(s, _):
+            scopy(s, part).start()
+            return 0
+
+        lax.fori_loop(1, nchip, ssend, 0)
+
+    l_up.wait()
     coarse = jnp.zeros((48, 512), F32)
     for a in range(2):
         for b in range(2):
@@ -226,20 +286,6 @@
     lax.fori_loop(1, nchan, psend, 0)
     PR[c + 1] = PS[c]
 
-    xcopy.wait_recv()
-    T[core] = T[core] + XR[...].astype(F32)
-    SS[...] = T[core].astype(BF16)
-
-    def scopy(s):
-        d = lax.rem(chip + s, nchip)
-        return remote(SS.at[d], SR.at[chip], ss.at[d], sr.at[chip], g, 2 * d + core)
-
-    def ssend(s, _):
-        scopy(s).start()
-        return 0
-
-    lax.fori_loop(1, nchip, ssend, 0)
-
     for w in wcopies:
         w.wait_recv()
 
@@ -277,27 +323,55 @@
     lax.fori_loop(1, nchan, fsend, 0)
     FR[c] = FS[c]
 
-    total = T[core, chip]
-
-    def srecv(s, acc):
-        o = lax.rem(chip + s, nchip)
-        remote(SS.at[o], SR.at[o], ss.at[o], sr.at[o], g, 2 * o + core).wait_recv()
-        return acc + SR[o].astype(F32)
-
-    total = lax.fori_loop(1, nchip, srecv, total)
-    flipped = jnp.concatenate([total, jnp.zeros((32, 128), F32)], axis=0).T
-    VT[...] = flipped.reshape(VT.shape)
-    YS[...] = flipped.astype(BF16).reshape(YS.shape)
-
-    def ycopy(s):
-        d = lax.rem(y + s, ny)
-        return remote(YS.at[d], YR.at[y], ys.at[d], yr.at[y], d * ZHI + zh, c)
-
-    def ysend(s, _):
-        ycopy(s).start()
-        return 0
-
-    lax.fori_loop(1, ny, ysend, 0)
+    for part in range(2):
+        low_row, count = (0, 128) if part == 0 else (128, 96)
+        total = T[core, chip, low_row:low_row + count, :]
+
+        def srecv(s, acc):
+            o = lax.rem(chip + s, nchip)
+            rows = pl.ds(low_row, count)
+            remote(
+                SS.at[o, rows], SR.at[o, rows], ss.at[part, o], sr.at[part, o], g, 2 * o + core
+            ).wait_recv()
+            return acc + SR[o, low_row:low_row + count, :].astype(F32)
+
+        total = lax.fori_loop(1, nchip, srecv, total)
+        if count < 128:
+            total = jnp.concatenate([total, jnp.zeros((128 - count, 128), F32)], axis=0)
+        flipped = total.T
+        VT[part] = flipped.reshape(VT.shape[1:])
+        YS[part] = flipped.astype(BF16).reshape(YS.shape[1:])
+
+        def ysend(s, _):
+            ycopy(s, part).start()
+            return 0
+
+        lax.fori_loop(1, ny, ysend, 0)
+
+    halves = []
+    for part in range(2):
+
+        def yrecv(s, acc):
+            o = lax.rem(y + s, ny)
+            remote(
+                YS.at[part, o], YR.at[part, o], ys.at[part, o], yr.at[part, o], o * ZHI + zh, c
+            ).wait_recv()
+            return acc + YR[part, o].astype(F32)
+
+        halves.append(lax.fori_loop(1, ny, yrecv, VT[part, y]))
+    v2 = jnp.concatenate(halves, axis=1)
+    for q in range(ZHI):
+        ZS[q] = jnp.concatenate([v2[4 * q:4 * q + 4], jnp.zeros((4, 256), F32)], axis=0)
+
+    def zcopy(s):
+        d = lax.rem(zh + s, ZHI)
+        return remote(ZS.at[d], ZR.at[zh], zs.at[d], zr.at[zh], y * ZHI + d, c)
+
+    def zsend(s, _):
+        zcopy(s).start()
+        return 0
+
+    lax.fori_loop(1, ZHI, zsend, 0)
 
     def frecv(s, _):
         o = group_of(s)
@@ -311,24 +385,36 @@
             acc = acc + FR[2 * p + k].astype(F32)
         gh_out[k * 16:(k + 1) * 16, :] = acc.astype(BF16)
 
-    def yrecv(s, acc):
-        o = lax.rem(y + s, ny)
-        remote(YS.at[o], YR.at[o], ys.at[o], yr.at[o], o * ZHI + zh, c).wait_recv()
-        return acc + YR[o].astype(F32)
-
-    v2 = lax.fori_loop(1, ny, yrecv, VT[y])
-    for q in range(ZHI):
-        ZS[q] = jnp.concatenate([v2[4 * q:4 * q + 4], jnp.zeros((4, 256), F32)], axis=0)
-
-    def zcopy(s):
-        d = lax.rem(zh + s, ZHI)
-        return remote(ZS.at[d], ZR.at[zh], zs.at[d], zr.at[zh], y * ZHI + d, c)
-
-    def zsend(s, _):
-        zcopy(s).start()
-        return 0
-
-    lax.fori_loop(1, ZHI, zsend, 0)
+    for h in near + far:
+        h.wait_send()
+    for w in wcopies:
+        w.wait_send()
+    for x in xcopies:
+        x.wait_send()
+
+    def sent_group(s, _):
+        pcopy(s).wait_send()
+        fcopy(s).wait_send()
+        return 0
+
+    def sent_chip(s, _):
+        scopy(s, 0).wait_send()
+        scopy(s, 1).wait_send()
+        return 0
+
+    def sent_y(s, _):
+        ycopy(s, 0).wait_send()
+        ycopy(s, 1).wait_send()
+        return 0
+
+    def sent_z(s, _):
+        zcopy(s).wait_send()
+        return 0
+
+    lax.fori_loop(1, nchan, sent_group, 0)
+    lax.fori_loop(1, nchip, sent_chip, 0)
+    lax.fori_loop(1, ny, sent_y, 0)
+    lax.fori_loop(1, ZHI, sent_z, 0)
 
     def zrecv(s, acc):
         o = lax.rem(zh + s, ZHI)
@@ -338,34 +424,6 @@
     v3 = lax.fori_loop(1, ZHI, zrecv, ZS[zh])
     for t in range(27):
         tg_out[t] = v3[0:4, 8 * t:8 * t + 8]
-
-    for h in halos:
-        h.wait_send()
-    for w in wcopies:
-        w.wait_send()
-    xcopy.wait_send()
-
-    def sent_group(s, _):
-        pcopy(s).wait_send()
-        fcopy(s).wait_send()
-        return 0
-
-    def sent_chip(s, _):
-        scopy(s).wait_send()
-        return 0
-
-    def sent_y(s, _):
-        ycopy(s).wait_send()
-        return 0
-
-    def sent_z(s, _):
-        zcopy(s).wait_send()
-        return 0
-
-    lax.fori_loop(1, nchan, sent_group, 0)
-    lax.fori_loop(1, nchip, sent_chip, 0)
-    lax.fori_loop(1, ny, sent_y, 0)
-    lax.fori_loop(1, ZHI, sent_z, 0)
 
 
 def body(grad_out, feat_full, filters_full, upsample_weight, filters_half):
@@ -403,19 +461,20 @@
             V((3, nchan + 2, 16, 256), BF16),
             V((nchan, 16, wide), BF16),
             V((nchan, 16, wide), BF16),
-            V((ny, 16, 256), F32),
-            V((ny, 16, 256), BF16),
-            V((ny, 16, 256), BF16),
+            V((2, ny, 16, 128), F32),
+            V((2, ny, 16, 128), BF16),
+            V((2, ny, 16, 128), BF16),
             V((ZHI, 8, 256), F32),
             V((ZHI, 8, 256), F32),
             D((7,)),
             D((9,)), D((9,)),
+            D((9,)), D((9,)),
             D((3,)), D((3,)),
-            D, D,
-            D((nchip,)), D((nchip,)),
+            D((3,)), D((3,)),
+            D((2, nchip)), D((2, nchip)),
             D((nchan,)), D((nchan,)),
             D((nchan,)), D((nchan,)),
-            D((ny,)), D((ny,)),
+            D((2, ny)), D((2, ny)),
             D((ZHI,)), D((ZHI,)),
         ],
         compiler_params=pltpu.CompilerParams(collective_id=0, has_side_effects=True),

time: 46.3 us -> 47.1 us (1.017)
  the two profiles are of different devices: /device:TPU:6 before, /device:TPU:1 now
where the time goes in v2:
time: 47.1 us; the launch traced here: 46.9 us
  Pallas kernels  44.2 us (94%)
  local copies, waits for them, and re-layouts  2.02 us (4%)
  between operations  0.65 us (1%)
    pallas_call x1, Pallas kernels, body(): pl.pallas_call(kernel, out_shape=(jax.ShapeDtypeStruct((32, wide), BF16),...  44.2 us
    unnamed x4, local copies, waits for them, and re-layouts  2.02 us

profile of v2, /device:TPU:1, one launch (start us, length us, event | category | flops | bytes accessed | tf_op | source)
XLA Modules:
  0.0 46.9 jit_solution(8817175967091879858)
XLA Ops:
  0.6 44.2 %shard_map.68 = (bf16[32,512]{1,0:T(8,128)(2,1)}, f32[27,4,8]{2,1,0:T(4,128)}) custom-call(bf16[8,2,16,128]{3,2,1,0:T(8,128)(2,1)} %go.1, bf16[8,2,16,128]{3,2,1,0:T(8,128)(2,1)} %fe.1, bf16[3,3,3,128,128]{4,3,2,1,0:T(8,128)(2,1)} %wf.1, bf16[2,2,2,512,128]{4,3,2,1,0:T(8,128)(2,1)} %uw.1, bf16[3,3,3,32,512]{4,3,2,1,0:T(8,128)(2,1)} %bitcast.3), custom_call_target="tpu_custom_call" | custom-call | tf_op jit(solution)/shard_map/pallas_call | solution.py:439
  44.9 0.0 copy-start
  44.9 1.4 %copy.9 = bf16[1,4,8,512]{3,2,1,0:T(8,128)(2,1)} copy(bf16[1,4,8,512]{3,2,1,0:T(8,128)(2,1)} %bitcast.5) | data formatting | bytes 65536
  46.3 0.0 copy-done
  46.3 0.6 %copy.10 = f32[3,3,3,4,8]{4,3,2,1,0:T(4,128)} copy(f32[3,3,3,4,8]{4,3,2,1,0:T(4,128)S(1)} %bitcast.4) | data formatting | bytes 6912
Async XLA Ops:
  44.9 1.4 %copy-start = (f32[27,4,8]{2,1,0:T(4,128)S(1)}, f32[27,4,8]{2,1,0:T(4,128)}, u32[]{:S(2)}) copy-start(f32[27,4,8]{2,1,0:T(4,128)} %get-tuple-element.5) | copy-start | bytes 10372

commit v3 on v2

--- a/solution.py
+++ b/solution.py
@@ -5,6 +5,7 @@
 from jax.experimental.pallas import tpu as pltpu
 from jax.sharding import PartitionSpec as P
 
+TAP_ROW = {1: 0, 0: 80, 2: 152}
 F32 = jnp.float32
 BF16 = jnp.bfloat16
 MESH = pl.DeviceIdType.MESH
@@ -40,6 +41,8 @@
             device_id=dev(gi, ci), device_id_type=MESH,
         )
 
+    other = c + 1 - 2 * core
+
     def group_of(s):
         return lax.rem(c + s, nchan)
 
@@ -49,16 +52,53 @@
     def zgrp(s):
         return y * ZHI + lax.rem(zh + s, ZHI)
 
-    def ycopy(s, part):
+    def ycopy(s):
         d = lax.rem(y + s, ny)
+        return remote(YS.at[d], YR.at[y], ys.at[d], yr.at[y], d * ZHI + zh, c)
+
+    def scopy(s, part):
+        d = lax.rem(chip + s, nchip)
+        rows = pl.ds(0, 80) if part == 0 else pl.ds(80, 144)
         return remote(
-            YS.at[part, d], YR.at[part, y], ys.at[part, d], yr.at[part, y], d * ZHI + zh, c
+            SS.at[d, rows], SR.at[chip, rows], ss.at[part, d], sr.at[part, chip], g, 2 * d + core
         )
+
+    def tap_sums(tx):
+        window = jnp.concatenate(
+            [G[4 - tx:12 - tx, 2 - ty:4 - ty].reshape(256, 128) for ty in range(3)], axis=1
+        )
+        part = lax.dot_general(window, feat3, TN, preferred_element_type=F32)
+        for ty in range(3):
+            rows = part[ty * 128:(ty + 1) * 128].reshape(nchip, 2, 8, 384)
+            for tz in range(3):
+                at = TAP_ROW[tx] + (ty * 3 + tz) * 8
+                for k in range(2):
+                    T[k, :, at:at + 8, :] = rows[:, k, :, tz * 128:(tz + 1) * 128]
+
+    def to_partner(part):
+        rows = slice(0, 80) if part == 0 else slice(80, 224)
+        XS[:, rows, :] = T[1 - core, :, rows, :].astype(BF16)
+        copy = remote(XS.at[:, rows, :], XR.at[:, rows, :], xs.at[part], xr.at[part], g, other)
+        copy.start()
+        return copy
+
+    def to_owners(copy, part):
+        rows = slice(0, 80) if part == 0 else slice(80, 224)
+        copy.wait_recv()
+        summed = T[core, :, rows, :] + XR[:, rows, :].astype(F32)
+        T[core, :, rows, :] = summed
+        SS[:, rows, :] = summed.astype(BF16)
+
+        def ssend(s, _):
+            scopy(s, part).start()
+            return 0
+
+        lax.fori_loop(1, nchip, ssend, 0)
 
     l_go = pltpu.make_async_copy(go, G.at[3:11, 1:3], lsem.at[0])
     l_wh = [
         pltpu.make_async_copy(
-            wh.at[t], WP.at[:, :, pl.ds(pl.multiple_of(t * 64 + core * 32, 32), 32), :], lsem.at[1 + t]
+            wh.at[t], WP.at[:, :, pl.ds(pl.multiple_of((2 - t) * 64 + core * 32, 32), 32), :], lsem.at[1 + t]
         )
         for t in range(3)
     ]
@@ -99,7 +139,7 @@
     PR[0] = jnp.zeros(PR.shape[1:], BF16)
     PR[nchan + 1] = jnp.zeros(PR.shape[1:], BF16)
     WP[:, :, 192:256, :] = jnp.zeros((3, 3, 64, WP.shape[3]), BF16)
-    T[:, :, 216:224, :] = jnp.zeros((2, nchip, 8, 128), F32)
+    T[:, :, 72:80, :] = jnp.zeros((2, nchip, 8, 128), F32)
     l_fe.wait()
     feat = FE[...].reshape(256, 128).astype(F32)
     z_of = lax.broadcasted_iota(jnp.int32, (256, 128), 0) % 16
@@ -129,7 +169,7 @@
     far_dst = {1: (0, 2), 2: (12, 14)}
     near = [
         halo(a, b, near_src[a], near_dst[a], hs, hr)
-        for a, b in ((1, 1), (1, 2), (2, 1), (2, 2), (1, 0), (2, 0), (0, 1), (0, 2))
+        for a, b in ((0, 1), (0, 2), (1, 1), (1, 2), (2, 1), (2, 2), (1, 0), (2, 0))
     ]
     far = [
         halo(a, b, far_src[a], far_dst[a], hs2, hr2)
@@ -139,14 +179,28 @@
         h.start()
     for h in far:
         h.start()
-    other = c + 1 - 2 * core
     wcopies = []
     for t in range(3):
         l_wh[t].wait()
-        rows = WP.at[:, :, pl.ds(pl.multiple_of(t * 64 + core * 32, 32), 32), :]
+        rows = WP.at[:, :, pl.ds(pl.multiple_of((2 - t) * 64 + core * 32, 32), 32), :]
         wcopies.append(remote(rows, rows, ws.at[t], wr.at[t], g, other))
         wcopies[-1].start()
-    for h in near:
+    near[0].wait_recv()
+    near[1].wait_recv()
+
+    @pl.when(c == 0)
+    def _():
+        G[3:11, 0:1] = jnp.zeros((8, 1, 16, 128), BF16)
+
+    @pl.when(c == nchan - 1)
+    def _():
+        G[3:11, 3:4] = jnp.zeros((8, 1, 16, 128), BF16)
+
+    tap_sums(1)
+    xcopy0 = to_partner(0)
+    to_owners(xcopy0, 0)
+
+    for h in near[2:]:
         h.wait_recv()
 
     @pl.when(g == 0)
@@ -159,28 +213,17 @@
 
     @pl.when(c == 0)
     def _():
-        G[2:12, 0:1] = jnp.zeros((10, 1, 16, 128), BF16)
+        G[2:3, 0:1] = jnp.zeros((1, 1, 16, 128), BF16)
+        G[11:12, 0:1] = jnp.zeros((1, 1, 16, 128), BF16)
 
     @pl.when(c == nchan - 1)
     def _():
-        G[2:12, 3:4] = jnp.zeros((10, 1, 16, 128), BF16)
-
-    xcopies = []
-    for tx in range(3):
-        window = jnp.concatenate(
-            [G[4 - tx:12 - tx, 2 - ty:4 - ty].reshape(256, 128) for ty in range(3)], axis=1
-        )
-        part = lax.dot_general(window, feat3, TN, preferred_element_type=F32)
-        for ty in range(3):
-            rows = part[ty * 128:(ty + 1) * 128].reshape(nchip, 2, 8, 384)
-            for tz in range(3):
-                at = ((tx * 3 + ty) * 3 + tz) * 8
-                for k in range(2):
-                    T[k, :, at:at + 8, :] = rows[:, k, :, tz * 128:(tz + 1) * 128]
-        part_rows = pl.ds(tx * 72, 80 if tx == 2 else 72)
-        XS[:, part_rows, :] = T[1 - core, :, part_rows, :].astype(BF16)
-        xcopies.append(remote(XS.at[:, part_rows, :], XR.at[:, part_rows, :], xs.at[tx], xr.at[tx], g, other))
-        xcopies[-1].start()
+        G[2:3, 3:4] = jnp.zeros((1, 1, 16, 128), BF16)
+        G[11:12, 3:4] = jnp.zeros((1, 1, 16, 128), BF16)
+
+    tap_sums(0)
+    tap_sums(2)
+    xcopy1 = to_partner(1)
 
     l_wf.wait()
     for h in far:
@@ -220,26 +263,6 @@
     up = jnp.where(z_at < 15, pltpu.roll(grown[:, 0:128], 383, 0), 0.0)
     down = jnp.where(z_at > 0, pltpu.roll(grown[:, 256:384], 1, 0), 0.0)
     IG[...] = grown[:, 128:256] + up + down
-
-    for x in xcopies:
-        x.wait_recv()
-    T[core] = T[core] + XR[...].astype(F32)
-    SS[...] = T[core].astype(BF16)
-
-    def scopy(s, part):
-        d = lax.rem(chip + s, nchip)
-        rows = pl.ds(0, 128) if part == 0 else pl.ds(128, 96)
-        return remote(
-            SS.at[d, rows], SR.at[chip, rows], ss.at[part, d], sr.at[part, chip], g, 2 * d + core
-        )
-
-    for part in range(2):
-
-        def ssend(s, _):
-            scopy(s, part).start()
-            return 0
-
-        lax.fori_loop(1, nchip, ssend, 0)
 
     l_up.wait()
     coarse = jnp.zeros((48, 512), F32)
@@ -268,11 +291,10 @@
             same, swap = (block, turned) if half == 0 else (turned, block)
             d = 2 * q + half
             for k in range(2):
-                pair = []
-                for i in (2 * k, 2 * k + 1):
-                    s0, s1, s2 = (i + 2) * 8, (i + 1) * 8, i * 8
-                    first = jnp.where(low, same[s0:s0 + 8], swap[s1:s1 + 8])
-                    pair.append(jnp.concatenate([first, same[s2:s2 + 8]], axis=1))
+                at = [coarse_row * 8 for coarse_row in range(2 * k, 2 * k + 4)]
+                pair = [
+                    jnp.where(low, same[at[r]:at[r] + 8], swap[at[r + 1]:at[r + 1] + 8]) for r in (0, 2)
+                ]
                 PS[2 * d + k] = jnp.concatenate(pair, axis=0).astype(BF16)
 
     def pcopy(s):
@@ -285,6 +307,7 @@
 
     lax.fori_loop(1, nchan, psend, 0)
     PR[c + 1] = PS[c]
+    to_owners(xcopy1, 1)
 
     for w in wcopies:
         w.wait_recv()
@@ -295,12 +318,18 @@
         return 0
 
     lax.fori_loop(1, nchan, precv, 0)
-    rows = (nchan + 2) * 16
-    slab = PR[...].reshape(rows, 256).astype(F32)
+    rows = (nchan + 2) * 8
+    slab = PR[...].astype(F32)
+    slab = jnp.concatenate([slab[:, 0:8, :], slab[:, 8:16, :]], axis=2).reshape(rows, 256)
     k_of = lax.broadcasted_iota(jnp.int32, (rows, 256), 0) % 8
-    SA[0] = jnp.where(k_of < 7, pltpu.roll(slab, rows - 1, 0), 0.0).astype(BF16).reshape(SA.shape[1:])
-    SA[1] = PR[...]
-    SA[2] = jnp.where(k_of > 0, pltpu.roll(slab, 1, 0), 0.0).astype(BF16).reshape(SA.shape[1:])
+    shifted = (
+        jnp.where(k_of < 7, pltpu.roll(slab, rows - 1, 0), 0.0),
+        slab,
+        jnp.where(k_of > 0, pltpu.roll(slab, 1, 0), 0.0),
+    )
+    for tz in range(3):
+        pair = [v.reshape(nchan + 2, 8, 256) for v in (shifted[tz], pltpu.roll(shifted[tz], 192, 1))]
+        SA[tz] = jnp.concatenate(pair, axis=1).astype(BF16)
     lhs = jnp.concatenate(
         [
             SA[tz, 2 - ty:2 - ty + nchan].reshape(nchan * 16, 256)
@@ -323,9 +352,9 @@
     lax.fori_loop(1, nchan, fsend, 0)
     FR[c] = FS[c]
 
+    sums = []
     for part in range(2):
-        low_row, count = (0, 128) if part == 0 else (128, 96)
-        total = T[core, chip, low_row:low_row + count, :]
+        low_row, count = (0, 80) if part == 0 else (80, 144)
 
         def srecv(s, acc):
             o = lax.rem(chip + s, nchip)
@@ -335,31 +364,23 @@
             ).wait_recv()
             return acc + SR[o, low_row:low_row + count, :].astype(F32)
 
-        total = lax.fori_loop(1, nchip, srecv, total)
-        if count < 128:
-            total = jnp.concatenate([total, jnp.zeros((128 - count, 128), F32)], axis=0)
-        flipped = total.T
-        VT[part] = flipped.reshape(VT.shape[1:])
-        YS[part] = flipped.astype(BF16).reshape(YS.shape[1:])
-
-        def ysend(s, _):
-            ycopy(s, part).start()
-            return 0
-
-        lax.fori_loop(1, ny, ysend, 0)
-
-    halves = []
-    for part in range(2):
-
-        def yrecv(s, acc):
-            o = lax.rem(y + s, ny)
-            remote(
-                YS.at[part, o], YR.at[part, o], ys.at[part, o], yr.at[part, o], o * ZHI + zh, c
-            ).wait_recv()
-            return acc + YR[part, o].astype(F32)
-
-        halves.append(lax.fori_loop(1, ny, yrecv, VT[part, y]))
-    v2 = jnp.concatenate(halves, axis=1)
+        sums.append(lax.fori_loop(1, nchip, srecv, T[core, chip, low_row:low_row + count, :]))
+    flipped = jnp.concatenate(sums + [jnp.zeros((32, 128), F32)], axis=0).T
+    VT[...] = flipped.reshape(VT.shape)
+    YS[...] = flipped.astype(BF16).reshape(YS.shape)
+
+    def ysend(s, _):
+        ycopy(s).start()
+        return 0
+
+    lax.fori_loop(1, ny, ysend, 0)
+
+    def yrecv(s, acc):
+        o = lax.rem(y + s, ny)
+        remote(YS.at[o], YR.at[o], ys.at[o], yr.at[o], o * ZHI + zh, c).wait_recv()
+        return acc + YR[o].astype(F32)
+
+    v2 = lax.fori_loop(1, ny, yrecv, VT[y])
     for q in range(ZHI):
         ZS[q] = jnp.concatenate([v2[4 * q:4 * q + 4], jnp.zeros((4, 256), F32)], axis=0)
 
@@ -389,8 +410,8 @@
         h.wait_send()
     for w in wcopies:
         w.wait_send()
-    for x in xcopies:
-        x.wait_send()
+    xcopy0.wait_send()
+    xcopy1.wait_send()
 
     def sent_group(s, _):
         pcopy(s).wait_send()
@@ -403,8 +424,7 @@
         return 0
 
     def sent_y(s, _):
-        ycopy(s, 0).wait_send()
-        ycopy(s, 1).wait_send()
+        ycopy(s).wait_send()
         return 0
 
     def sent_z(s, _):
@@ -422,8 +442,10 @@
         return acc + ZR[o]
 
     v3 = lax.fori_loop(1, ZHI, zrecv, ZS[zh])
-    for t in range(27):
-        tg_out[t] = v3[0:4, 8 * t:8 * t + 8]
+    for tx in range(3):
+        for t in range(9):
+            at = TAP_ROW[tx] + 8 * t
+            tg_out[tx * 9 + t] = v3[0:4, at:at + 8]
 
 
 def body(grad_out, feat_full, filters_full, upsample_weight, filters_half):
@@ -439,8 +461,8 @@
     grad_half, taps = pl.pallas_call(
         kernel,
         out_shape=(
-            jax.ShapeDtypeStruct((32, wide), BF16),
-            jax.ShapeDtypeStruct((27, 4, 8), F32),
+            pltpu.VMEM((32, wide), BF16),
+            pltpu.VMEM((27, 4, 8), F32),
         ),
         in_specs=[anyspace] * 5,
         out_specs=(vmem, vmem),
@@ -456,25 +478,25 @@
             V((nchip, 224, 128), BF16),
             V((nchip, 224, 128), BF16),
             V((nchip, 224, 128), BF16),
-            V((nchan, 16, 256), BF16),
-            V((nchan + 2, 16, 256), BF16),
+            V((nchan, 16, 128), BF16),
+            V((nchan + 2, 16, 128), BF16),
             V((3, nchan + 2, 16, 256), BF16),
             V((nchan, 16, wide), BF16),
             V((nchan, 16, wide), BF16),
-            V((2, ny, 16, 128), F32),
-            V((2, ny, 16, 128), BF16),
-            V((2, ny, 16, 128), BF16),
+            V((ny, 16, 256), F32),
+            V((ny, 16, 256), BF16),
+            V((ny, 16, 256), BF16),
             V((ZHI, 8, 256), F32),
             V((ZHI, 8, 256), F32),
             D((7,)),
             D((9,)), D((9,)),
             D((9,)), D((9,)),
             D((3,)), D((3,)),
-            D((3,)), D((3,)),
+            D((2,)), D((2,)),
             D((2, nchip)), D((2, nchip)),
             D((nchan,)), D((nchan,)),
             D((nchan,)), D((nchan,)),
-            D((2, ny)), D((2, ny)),
+            D((ny,)), D((ny,)),
             D((ZHI,)), D((ZHI,)),
         ],
         compiler_params=pltpu.CompilerParams(collective_id=0, has_side_effects=True),

time: 47.1 us -> 41.7 us (0.89)
  the two profiles are of different devices: /device:TPU:1 before, /device:TPU:6 now
where the time goes in v3:
time: 41.7 us; the launch traced here: 41.5 us
  Pallas kernels  39.7 us (95%)
  local copies, waits for them, and re-layouts  1.24 us (3%)
  between operations  0.64 us (2%)
    pallas_call x1, Pallas kernels, body(): pl.pallas_call(kernel, out_shape=(pltpu.VMEM((32, wide), BF16), pltpu.VME...  39.7 us
    unnamed x2, local copies, waits for them, and re-layouts  1.24 us

profile of v3, /device:TPU:6, one launch (start us, length us, event | category | flops | bytes accessed | tf_op | source)
XLA Modules:
  0.0 41.5 jit_solution(14987971008469700876)
XLA Ops:
  0.6 39.7 %shard_map.68 = (bf16[32,512]{1,0:T(8,128)(2,1)S(1)}, f32[27,4,8]{2,1,0:T(4,128)S(1)}) custom-call(bf16[8,2,16,128]{3,2,1,0:T(8,128)(2,1)} %go.1, bf16[8,2,16,128]{3,2,1,0:T(8,128)(2,1)} %fe.1, bf16[3,3,3,128,128]{4,3,2,1,0:T(8,128)(2,1)} %wf.1, bf16[2,2,2,512,128]{4,3,2,1,0:T(8,128)(2,1)} %uw.1, bf16[3,3,3,32,512]{4,3,2,1,0:T(8,128)(2,1)} %bitcast.5), custom_call_target="tpu_custom_call" | custom-call | tf_op jit(solution)/shard_map/pallas_call | solution.py:461
  40.3 0.6 %copy.9 = bf16[1,4,8,512]{3,2,1,0:T(8,128)(2,1)} copy(bf16[1,4,8,512]{3,2,1,0:T(8,128)(2,1)S(1)} %bitcast.4) | data formatting | bytes 65536
  40.9 0.6 %copy.10 = f32[3,3,3,4,8]{4,3,2,1,0:T(4,128)} copy(f32[3,3,3,4,8]{4,3,2,1,0:T(4,128)S(1)} %bitcast.3) | data formatting | bytes 6912

commit v4 on v1

v4 whole, which is shorter than its diff:
```python
import jax
import jax.numpy as jnp
from jax import lax
from jax.experimental import pallas as pl
from jax.experimental.pallas import tpu as pltpu
from jax.sharding import PartitionSpec as P

TAP_ROW = {1: 0, 0: 80, 2: 152}
F32 = jnp.float32
BF16 = jnp.bfloat16
MESH = pl.DeviceIdType.MESH
NT = (((1,), (1,)), ((), ()))
TN = (((0,), (0,)), ((), ()))
ZHI = 4


def kernel(
    go, fe, wf, uw, wh,
    gh_out, tg_out,
    G, FE, F3, WF, UP, WP, IG,
    T, XS, XR, SS, SR,
    PS, PR, SA, FS, FR,
    VT, YS, YR, ZS, ZR,
    lsem, es, er, ns, nr, qs, qr, rs, rr, ws, wr, xs, xr, ss, sr, ps, pr, fs, fr, ys, yr, zs, zr,
):
    g = lax.axis_index("grp")
    c = lax.axis_index("chan")
    ngrp = lax.axis_size("grp")
    nchan = lax.axis_size("chan")
    nchip = nchan // 2
    ny = ngrp // ZHI
    y, zh = g // ZHI, lax.rem(g, ZHI)
    chip, core = c // 2, lax.rem(c, 2)

    def dev(gi, ci):
        return {"grp": gi, "chan": ci}

    def remote(src, dst, send, recv, gi, ci):
        return pltpu.make_async_remote_copy(
            src_ref=src, dst_ref=dst, send_sem=send, recv_sem=recv,
            device_id=dev(gi, ci), device_id_type=MESH,
        )

    other = c + 1 - 2 * core

    def group_of(s):
        return lax.rem(c + s, nchan)

    def ygrp(s):
        return lax.rem(y + s, ny) * ZHI + zh

    def zgrp(s):
        return y * ZHI + lax.rem(zh + s, ZHI)

    def sent(ref, sem):
        remote(ref, ref, sem, sem, g, other).wait_send()

    def arrived(ref, sem):
        remote(ref, ref, sem, sem, g, other).wait_recv()

    def ycopy(s):
        d = lax.rem(y + s, ny)
        return remote(YS.at[d], YR.at[y], ys, yr, d * ZHI + zh, c)

    def tap_rows(part):
        return slice(0, 80) if part == 0 else slice(80, 224)

    def tap_sums(txs, feat3):
        planes = []
        for tx in txs:
            if tx == 0:
                last = jnp.where(g == ngrp - 1, jnp.zeros((1, 2, 16, 128), BF16), G[11:12, 1:3])
                window = jnp.concatenate([G[4:11, 1:3], last], axis=0)
            elif tx == 1:
                window = G[3:11, 1:3]
            else:
                first = jnp.where(g == 0, jnp.zeros((1, 2, 16, 128), BF16), G[2:3, 1:3])
                window = jnp.concatenate([first, G[3:10, 1:3]], axis=0)
            planes.append(window.reshape(256, 128))
        part = lax.dot_general(
            jnp.concatenate(planes, axis=1), feat3, TN, preferred_element_type=F32
        )
        for n, tx in enumerate(txs):
            rows = part[n * 128:(n + 1) * 128].reshape(nchip, 2, 8, 9 * 128)
            for t in range(9):
                at = TAP_ROW[tx] + t * 8
                for k in range(2):
                    T[k, :, at:at + 8, :] = rows[:, k, :, t * 128:(t + 1) * 128]

    def to_partner(part):
        rows = tap_rows(part)
        XS[:, rows, :] = T[1 - core, :, rows, :].astype(BF16)
        remote(XS.at[:, rows, :], XR.at[:, rows, :], xs.at[part], xr.at[part], g, other).start()

    def to_owners(part):
        rows = tap_rows(part)
        arrived(XR.at[:, rows, :], xr.at[part])
        summed = T[core, :, rows, :] + XR[:, rows, :].astype(F32)
        T[core, :, rows, :] = summed
        SS[:, rows, :] = summed.astype(BF16)

        def ssend(s, _):
            d = lax.rem(chip + s, nchip)
            remote(
                SS.at[d, rows], SR.at[chip, rows], ss.at[part], sr.at[part], g, 2 * d + core
            ).start()
            return 0

        lax.fori_loop(1, nchip, ssend, 0)

    def along_z(cells):
        z_of = lax.broadcasted_iota(jnp.int32, cells.shape, 0) % 16
        before = jnp.where(z_of > 0, pltpu.roll(cells, 1, 0), 0.0)
        after = jnp.where(z_of < 15, pltpu.roll(cells, cells.shape[0] - 1, 0), 0.0)
        return jnp.concatenate([before, cells, after], axis=1).astype(BF16)

    l_go = pltpu.make_async_copy(go, G.at[3:11, 1:3], lsem.at[0])
    l_fe = pltpu.make_async_copy(fe, FE.at[:, 1:3], lsem.at[1])
    own_rows = [WP.at[:, :, pl.ds(pl.multiple_of((2 - t) * 64 + core * 32, 32), 32), :] for t in range(3)]
    l_wh = [pltpu.make_async_copy(wh.at[t], own_rows[t], lsem.at[2 + t]) for t in range(3)]
    l_wf = pltpu.make_async_copy(wf, WF, lsem.at[5])
    l_up = pltpu.make_async_copy(uw, UP, lsem.at[6])
    l_fe.start()
    l_go.start()
    for t in range(3):
        l_wh[t].start()
    l_wf.start()
    l_up.start()

    barrier = pltpu.get_barrier_semaphore()

    def hello(gi, ci):
        pl.semaphore_signal(barrier, inc=1, device_id=dev(gi, ci), device_id_type=MESH)

    def hello_group(s, _):
        hello(g, group_of(s))
        return 0

    def hello_y(s, _):
        hello(ygrp(s), c)
        return 0

    def hello_z(s, _):
        hello(zgrp(s), c)
        return 0

    for dg in (1, ngrp - 1):
        hello(lax.rem(g + dg, ngrp), c)
    lax.fori_loop(1, ny, hello_y, 0)
    lax.fori_loop(1, ZHI, hello_z, 0)
    lax.fori_loop(1, nchan, hello_group, 0)

    PR[0] = jnp.zeros(PR.shape[1:], BF16)
    PR[nchan + 1] = jnp.zeros(PR.shape[1:], BF16)
    WP[:, :, 192:256, :] = jnp.zeros((3, 3, 64, WP.shape[3]), BF16)
    T[:, :, 72:80, :] = jnp.zeros((2, nchip, 8, 128), F32)
    l_fe.wait()
    F3[:, 1:3] = along_z(FE[:, 1:3].reshape(256, 128).astype(F32)).reshape(8, 2, 16, 384)
    l_go.wait()

    pl.semaphore_wait(barrier, (nchan - 1) + (ny - 1) + (ZHI - 1) + 2)

    upper, lower = lax.rem(g + 1, ngrp), lax.rem(g + ngrp - 1, ngrp)
    right, left = group_of(1), group_of(nchan - 1)
    remote(FE.at[:, 2:3], FE.at[:, 0:1], es, er, g, right).start()
    remote(FE.at[:, 1:2], FE.at[:, 3:4], es, er, g, left).start()
    remote(G.at[10:11, 1:3], G.at[2:3, 1:3], ns, nr, upper, c).start()
    remote(G.at[3:4, 1:3], G.at[11:12, 1:3], ns, nr, lower, c).start()
    remote(G.at[8:10, 1:3], G.at[0:2, 1:3], qs, qr, upper, c).start()
    remote(G.at[4:6, 1:3], G.at[12:14, 1:3], qs, qr, lower, c).start()
    remote(G.at[3:11, 2:3], G.at[3:11, 0:1], rs, rr, g, right).start()
    remote(G.at[3:11, 1:2], G.at[3:11, 3:4], rs, rr, g, left).start()
    arrived(FE.at[:, 1:3], er)
    for row, edge in ((0, 0), (3, nchan - 1)):
        shifted = along_z(FE[:, row:row + 1].reshape(128, 128).astype(F32)).reshape(8, 1, 16, 384)
        F3[:, row:row + 1] = jnp.where(c == edge, jnp.zeros_like(shifted), shifted)

    feat3 = jnp.concatenate([F3[:, ty:ty + 2].reshape(256, 384) for ty in range(3)], axis=1)
    tap_sums((1,), feat3)
    to_partner(0)
    arrived(G.at[0:1, 0:4], nr)
    tap_sums((0, 2), feat3)
    to_partner(1)
    arrived(G.at[0:2, 0:4], qr)
    for planes in ((0, 3), (11, 14)):
        at = slice(planes[0], planes[1])
        remote(G.at[at, 2:3], G.at[at, 0:1], rs, rr, g, right).start()
        remote(G.at[at, 1:2], G.at[at, 3:4], rs, rr, g, left).start()
    to_owners(0)
    for t in range(3):
        l_wh[t].wait()
        remote(own_rows[t], own_rows[t], ws, wr, g, other).start()
    to_owners(1)
    l_wf.wait()
    l_up.wait()
    sent(G.at[0:7, 0:4], rs)
    arrived(G.at[0:7, 0:4], rr)

    @pl.when(g == 0)
    def _():
        G[0:3] = jnp.zeros((3,) + G.shape[1:], BF16)

    @pl.when(g == ngrp - 1)
    def _():
        G[11:14] = jnp.zeros((3,) + G.shape[1:], BF16)

    @pl.when(c == 0)
    def _():
        G[:, 0:1] = jnp.zeros((14, 1, 16, 128), BF16)

    @pl.when(c == nchan - 1)
    def _():
        G[:, 3:4] = jnp.zeros((14, 1, 16, 128), BF16)

    lhs = jnp.concatenate(
        [
            G[2 - tx:14 - tx, 2 - ty:4 - ty].reshape(384, 128)
            for tx in range(3)
            for ty in range(3)
        ],
        axis=1,
    )
    rhs = jnp.concatenate(
        [WF[tx, ty].reshape(384, 128) for tx in range(3) for ty in range(3)], axis=1
    )
    grown = lax.dot_general(lhs, rhs, NT, preferred_element_type=F32)
    z_at = lax.broadcasted_iota(jnp.int32, (384, 128), 0) % 16
    up = jnp.where(z_at < 15, pltpu.roll(grown[:, 0:128], 383, 0), 0.0)
    down = jnp.where(z_at > 0, pltpu.roll(grown[:, 256:384], 1, 0), 0.0)
    IG[...] = grown[:, 128:256] + up + down

    coarse = jnp.zeros((48, 512), F32)
    for a in range(2):
        for b in range(2):
            cells = jnp.concatenate(
                [
                    jnp.concatenate(
                        [IG[pl.ds(((2 * i + a) * 2 + b) * 16 + k, 8, stride=2), :] for i in range(6)],
                        axis=0,
                    )
                    for k in range(2)
                ],
                axis=1,
            ).astype(BF16)
            weight = jnp.concatenate([UP[a, b, 0], UP[a, b, 1]], axis=1)
            coarse = coarse + lax.dot_general(cells, weight, NT, preferred_element_type=F32)
    row_of = lax.broadcasted_iota(jnp.int32, (48, 512), 0)
    outside = ((row_of < 8) & (g == 0)) | ((row_of >= 40) & (g == ngrp - 1))
    coarse = jnp.where(outside, 0.0, coarse)
    low = lax.broadcasted_iota(jnp.int32, (8, 128), 1) < 64
    for q in range(4):
        block = coarse[:, q * 128:(q + 1) * 128]
        turned = pltpu.roll(block, 64, 1)
        for half in range(2):
            same, swap = (block, turned) if half == 0 else (turned, block)
            d = 2 * q + half
            for k in range(2):
                at = [coarse_row * 8 for coarse_row in range(2 * k, 2 * k + 4)]
                pair = [
                    jnp.where(low, same[at[r]:at[r] + 8], swap[at[r + 1]:at[r + 1] + 8]) for r in (0, 2)
                ]
                PS[2 * d + k] = jnp.concatenate(pair, axis=0).astype(BF16)

    def psend(s, _):
        d = group_of(s)
        remote(PS.at[d], PR.at[c + 1], ps, pr, g, d).start()
        return 0

    lax.fori_loop(1, nchan, psend, 0)
    PR[c + 1] = PS[c]
    for part in range(2):
        arrived(SR.at[0:7, tap_rows(part)], sr.at[part])
    total = T[core, chip]
    for s in range(1, nchan // 2):
        total = total + SR[lax.rem(chip + s, nchip)].astype(F32)
    flipped = jnp.concatenate([total, jnp.zeros((32, 128), F32)], axis=0).T
    VT[...] = flipped.reshape(VT.shape)
    YS[...] = flipped.astype(BF16).reshape(YS.shape)

    def ysend(s, _):
        ycopy(s).start()
        return 0

    lax.fori_loop(1, ny, ysend, 0)

    arrived(WP.at[:, :, 0:96, :], wr)
    arrived(PR.at[0:15], pr)
    rows = (nchan + 2) * 8
    slab = PR[...].astype(F32)
    slab = jnp.concatenate([slab[:, 0:8, :], slab[:, 8:16, :]], axis=2).reshape(rows, 256)
    k_of = lax.broadcasted_iota(jnp.int32, (rows, 256), 0) % 8
    shifted = (
        jnp.where(k_of < 7, pltpu.roll(slab, rows - 1, 0), 0.0),
        slab,
        jnp.where(k_of > 0, pltpu.roll(slab, 1, 0), 0.0),
    )
    for tz in range(3):
        pair = [v.reshape(nchan + 2, 8, 256) for v in (shifted[tz], pltpu.roll(shifted[tz], 192, 1))]
        SA[tz] = jnp.concatenate(pair, axis=1).astype(BF16)
    lhs = jnp.concatenate(
        [
            SA[tz, 2 - ty:2 - ty + nchan].reshape(nchan * 16, 256)
            for ty in range(3)
            for tz in range(3)
        ],
        axis=1,
    )
    part = jnp.dot(lhs, WP[...].reshape(9 * 256, 512), preferred_element_type=F32)
    FS[...] = part.astype(BF16).reshape(FS.shape)

    def fsend(s, _):
        d = group_of(s)
        remote(FS.at[d], FR.at[c], fs, fr, g, d).start()
        return 0

    lax.fori_loop(1, nchan, fsend, 0)
    FR[c] = FS[c]

    arrived(YR.at[0:7], yr)
    v2 = VT[y]
    for s in range(1, YR.shape[0]):
        v2 = v2 + YR[lax.rem(y + s, ny)].astype(F32)
    for q in range(ZHI):
        ZS[q] = jnp.concatenate([v2[4 * q:4 * q + 4], jnp.zeros((4, 256), F32)], axis=0)

    def zsend(s, _):
        d = lax.rem(zh + s, ZHI)
        remote(ZS.at[d], ZR.at[zh], zs, zr, y * ZHI + d, c).start()
        return 0

    lax.fori_loop(1, ZHI, zsend, 0)

    arrived(FR.at[0:15], fr)
    for k in range(2):
        acc = FR[k].astype(F32)
        for p in range(1, nchan // 2):
            acc = acc + FR[2 * p + k].astype(F32)
        gh_out[k * 16:(k + 1) * 16, :] = acc.astype(BF16)

    sent(FE.at[:, 1:3], es)
    sent(G.at[0:1, 0:4], ns)
    sent(G.at[0:2, 0:4], qs)
    sent(WP.at[:, :, 0:96, :], ws)
    for part in range(2):
        sent(XS.at[:, tap_rows(part), :], xs.at[part])
        sent(SS.at[0:7, tap_rows(part)], ss.at[part])
    sent(PS.at[0:15], ps)
    sent(FS.at[0:15], fs)
    sent(YS.at[0:7], ys)
    sent(ZS.at[0:3], zs)

    arrived(ZR.at[0:3], zr)
    v3 = ZS[zh]
    for s in range(1, ZHI):
        v3 = v3 + ZR[lax.rem(zh + s, ZHI)]
    for tx in range(3):
        for t in range(9):
            at = TAP_ROW[tx] + 8 * t
            tg_out[tx * 9 + t] = v3[0:4, at:at + 8]


def body(grad_out, feat_full, filters_full, upsample_weight, filters_half):
    nchan = lax.axis_size("chan")
    ny = lax.axis_size("grp") // ZHI
    nchip = nchan // 2
    wide = filters_half.shape[3]
    turned = jnp.swapaxes(filters_half, 3, 4)
    V = pltpu.VMEM
    D = pltpu.SemaphoreType.DMA
    anyspace = pl.BlockSpec(memory_space=pl.ANY)
    vmem = pl.BlockSpec(memory_space=pltpu.VMEM)
    grad_half, taps = pl.pallas_call(
        kernel,
        out_shape=(
            pltpu.VMEM((32, wide), BF16),
            pltpu.VMEM((27, 4, 8), F32),
        ),
        in_specs=[anyspace] * 5,
        out_specs=(vmem, vmem),
        scratch_shapes=[
            V((14, 4, 16, 128), BF16),
            V((8, 4, 16, 128), BF16),
            V((8, 4, 16, 384), BF16),
            V((3, 3, 3, 128, 128), BF16),
            V((2, 2, 2, wide, 128), BF16),
            V((3, 3, 256, wide), BF16),
            V((384, 128), F32),
            V((2, nchip, 224, 128), F32),
            V((nchip, 224, 128), BF16),
            V((nchip, 224, 128), BF16),
            V((nchip, 224, 128), BF16),
            V((nchip, 224, 128), BF16),
            V((nchan, 16, 128), BF16),
            V((nchan + 2, 16, 128), BF16),
            V((3, nchan + 2, 16, 256), BF16),
            V((nchan, 16, wide), BF16),
            V((nchan, 16, wide), BF16),
            V((ny, 16, 256), F32),
            V((ny, 16, 256), BF16),
            V((ny, 16, 256), BF16),
            V((ZHI, 8, 256), F32),
            V((ZHI, 8, 256), F32),
            D((7,)),
            D, D, D, D, D, D, D, D, D, D,
            D((2,)), D((2,)), D((2,)), D((2,)),
            D, D, D, D, D, D, D, D,
        ],
        compiler_params=pltpu.CompilerParams(collective_id=0, has_side_effects=True),
    )(grad_out, feat_full, filters_full, upsample_weight, turned)
    return grad_half.reshape(1, 4, 8, wide), taps.reshape(3, 3, 3, 4, 8)


def solution(mesh):
    in_specs = (
        P("grp", "chan", None, None),
        P("grp", "chan", None, None),
        P(),
        P(),
        P(None, None, None, None, "chan"),
    )
    out_specs = (P("chan", "grp", None, None), P(None, None, None, "grp", "chan"))
    return jax.shard_map(body, mesh=mesh, in_specs=in_specs, out_specs=out_specs, check_vma=False)
```

time: 46.3 us -> 39.1 us (0.84)
  the two profiles are of different devices: /device:TPU:6 before, /device:TPU:1 now
where the time goes in v4:
time: 39.1 us; the launch traced here: 39 us
  Pallas kernels  37.1 us (95%)
  local copies, waits for them, and re-layouts  1.24 us (3%)
  between operations  0.64 us (2%)
    pallas_call x1, Pallas kernels, body(): pl.pallas_call(kernel, out_shape=(pltpu.VMEM((32, wide), BF16), pltpu.VME...  37.1 us
    unnamed x2, local copies, waits for them, and re-layouts  1.24 us

profile of v4, /device:TPU:1, one launch (start us, length us, event | category | flops | bytes accessed | tf_op | source)
XLA Modules:
  0.0 39.0 jit_solution(2409737274762256831)
XLA Ops:
  0.6 37.1 %shard_map.68 = (bf16[32,512]{1,0:T(8,128)(2,1)S(1)}, f32[27,4,8]{2,1,0:T(4,128)S(1)}) custom-call(bf16[8,2,16,128]{3,2,1,0:T(8,128)(2,1)} %go.1, bf16[8,2,16,128]{3,2,1,0:T(8,128)(2,1)} %fe.1, bf16[3,3,3,128,128]{4,3,2,1,0:T(8,128)(2,1)} %wf.1, bf16[2,2,2,512,128]{4,3,2,1,0:T(8,128)(2,1)} %uw.1, bf16[3,3,3,32,512]{4,3,2,1,0:T(8,128)(2,1)} %bitcast.5), custom_call_target="tpu_custom_call" | custom-call | tf_op jit(solution)/shard_map/pallas_call | solution.py:372
  37.8 0.6 %copy.9 = bf16[1,4,8,512]{3,2,1,0:T(8,128)(2,1)} copy(bf16[1,4,8,512]{3,2,1,0:T(8,128)(2,1)S(1)} %bitcast.4) | data formatting | bytes 65536
  38.4 0.6 %copy.10 = f32[3,3,3,4,8]{4,3,2,1,0:T(4,128)} copy(f32[3,3,3,4,8]{4,3,2,1,0:T(4,128)S(1)} %bitcast.3) | data formatting | bytes 6912

commit v5 on v4

--- a/solution.py
+++ b/solution.py
@@ -5,7 +5,6 @@
 from jax.experimental.pallas import tpu as pltpu
 from jax.sharding import PartitionSpec as P
 
-TAP_ROW = {1: 0, 0: 80, 2: 152}
 F32 = jnp.float32
 BF16 = jnp.bfloat16
 MESH = pl.DeviceIdType.MESH
@@ -18,10 +17,10 @@
     go, fe, wf, uw, wh,
     gh_out, tg_out,
     G, FE, F3, WF, UP, WP, IG,
-    T, XS, XR, SS, SR,
+    T, SS, SR,
     PS, PR, SA, FS, FR,
     VT, YS, YR, ZS, ZR,
-    lsem, es, er, ns, nr, qs, qr, rs, rr, ws, wr, xs, xr, ss, sr, ps, pr, fs, fr, ys, yr, zs, zr,
+    lsem, es, er, ns, nr, qs, qr, rs, rr, ws, wr, ss, sr, ps, pr, fs, fr, ys, yr, zs, zr,
 ):
     g = lax.axis_index("grp")
     c = lax.axis_index("chan")
@@ -63,59 +62,51 @@
         return remote(YS.at[d], YR.at[y], ys, yr, d * ZHI + zh, c)
 
     def tap_rows(part):
-        return slice(0, 80) if part == 0 else slice(80, 224)
-
-    def tap_sums(txs, feat3):
-        planes = []
-        for tx in txs:
-            if tx == 0:
-                last = jnp.where(g == ngrp - 1, jnp.zeros((1, 2, 16, 128), BF16), G[11:12, 1:3])
-                window = jnp.concatenate([G[4:11, 1:3], last], axis=0)
-            elif tx == 1:
-                window = G[3:11, 1:3]
+        return slice(0, 40) if part == 0 else slice(40, 112)
+
+    def tap_sums(tx, feat3):
+        if tx == 0:
+            last = jnp.where(g == ngrp - 1, jnp.zeros((1, 4, 16, 128), BF16), G[11:12, 1:5])
+            window = jnp.concatenate([G[4:11, 1:5], last], axis=0)
+        elif tx == 1:
+            window = G[3:11, 1:5]
+        else:
+            first = jnp.where(g == 0, jnp.zeros((1, 4, 16, 128), BF16), G[2:3, 1:5])
+            window = jnp.concatenate([first, G[3:10, 1:5]], axis=0)
+        part = lax.dot_general(window.reshape(512, 128), feat3, TN, preferred_element_type=F32)
+        rows = part.reshape(nchan, 8, 5 * 128)
+        for n in range(5):
+            if tx == 1:
+                at = n * 8
+            elif tx == 0:
+                at = 40 if n == 0 else pl.multiple_of((5 + n - core) * 8, 8)
             else:
-                first = jnp.where(g == 0, jnp.zeros((1, 2, 16, 128), BF16), G[2:3, 1:3])
-                window = jnp.concatenate([first, G[3:10, 1:3]], axis=0)
-            planes.append(window.reshape(256, 128))
-        part = lax.dot_general(
-            jnp.concatenate(planes, axis=1), feat3, TN, preferred_element_type=F32
-        )
-        for n, tx in enumerate(txs):
-            rows = part[n * 128:(n + 1) * 128].reshape(nchip, 2, 8, 9 * 128)
-            for t in range(9):
-                at = TAP_ROW[tx] + t * 8
-                for k in range(2):
-                    T[k, :, at:at + 8, :] = rows[:, k, :, t * 128:(t + 1) * 128]
-
-    def to_partner(part):
-        rows = tap_rows(part)
-        XS[:, rows, :] = T[1 - core, :, rows, :].astype(BF16)
-        remote(XS.at[:, rows, :], XR.at[:, rows, :], xs.at[part], xr.at[part], g, other).start()
+                at = pl.multiple_of((10 + n - core) * 8, 8)
+            T[:, pl.ds(at, 8), :] = rows[:, :, n * 128:(n + 1) * 128]
 
     def to_owners(part):
         rows = tap_rows(part)
-        arrived(XR.at[:, rows, :], xr.at[part])
-        summed = T[core, :, rows, :] + XR[:, rows, :].astype(F32)
-        T[core, :, rows, :] = summed
-        SS[:, rows, :] = summed.astype(BF16)
+        SS[:, rows, :] = T[:, rows, :].astype(BF16)
 
         def ssend(s, _):
-            d = lax.rem(chip + s, nchip)
-            remote(
-                SS.at[d, rows], SR.at[chip, rows], ss.at[part], sr.at[part], g, 2 * d + core
-            ).start()
+            d = group_of(s)
+            remote(SS.at[d, rows], SR.at[c, rows], ss.at[part], sr.at[part], g, d).start()
             return 0
 
-        lax.fori_loop(1, nchip, ssend, 0)
+        lax.fori_loop(1, nchan, ssend, 0)
 
     def along_z(cells):
         z_of = lax.broadcasted_iota(jnp.int32, cells.shape, 0) % 16
         before = jnp.where(z_of > 0, pltpu.roll(cells, 1, 0), 0.0)
         after = jnp.where(z_of < 15, pltpu.roll(cells, cells.shape[0] - 1, 0), 0.0)
-        return jnp.concatenate([before, cells, after], axis=1).astype(BF16)
-
-    l_go = pltpu.make_async_copy(go, G.at[3:11, 1:3], lsem.at[0])
-    l_fe = pltpu.make_async_copy(fe, FE.at[:, 1:3], lsem.at[1])
+        return before.astype(BF16), cells.astype(BF16), after.astype(BF16)
+
+    mine, theirs = pl.ds(1 + 2 * core, 2), pl.ds(3 - 2 * core, 2)
+    inner_row, edge_row = pl.ds(2 + core, 1), pl.ds(1 + 3 * core, 1)
+    far_row = pl.ds(5 - 5 * core, 1)
+    facing, beyond = group_of(nchan + 2 * core - 1), group_of(nchan + 4 * core - 2)
+    l_go = pltpu.make_async_copy(go, G.at[3:11, mine], lsem.at[0])
+    l_fe = pltpu.make_async_copy(fe, FE.at[:, mine], lsem.at[1])
     own_rows = [WP.at[:, :, pl.ds(pl.multiple_of((2 - t) * 64 + core * 32, 32), 32), :] for t in range(3)]
     l_wh = [pltpu.make_async_copy(wh.at[t], own_rows[t], lsem.at[2 + t]) for t in range(3)]
     l_wf = pltpu.make_async_copy(wf, WF, lsem.at[5])
@@ -146,6 +137,7 @@
 
     for dg in (1, ngrp - 1):
         hello(lax.rem(g + dg, ngrp), c)
+        hello(lax.rem(g + dg, ngrp), other)
     lax.fori_loop(1, ny, hello_y, 0)
     lax.fori_loop(1, ZHI, hello_z, 0)
     lax.fori_loop(1, nchan, hello_group, 0)
@@ -153,48 +145,58 @@
     PR[0] = jnp.zeros(PR.shape[1:], BF16)
     PR[nchan + 1] = jnp.zeros(PR.shape[1:], BF16)
     WP[:, :, 192:256, :] = jnp.zeros((3, 3, 64, WP.shape[3]), BF16)
-    T[:, :, 72:80, :] = jnp.zeros((2, nchip, 8, 128), F32)
+    def feature_rows(rows, count, edge):
+        cells = count * 128
+        for tz, shifted in enumerate(along_z(FE[:, rows].reshape(cells, 128).astype(F32))):
+            shifted = shifted.reshape(8, count, 16, 128)
+            if edge is not None:
+                shifted = jnp.where(chip == edge, jnp.zeros_like(shifted), shifted)
+            F3[tz, :, rows] = shifted
+
     l_fe.wait()
-    F3[:, 1:3] = along_z(FE[:, 1:3].reshape(256, 128).astype(F32)).reshape(8, 2, 16, 384)
+    feature_rows(mine, 2, None)
     l_go.wait()
 
-    pl.semaphore_wait(barrier, (nchan - 1) + (ny - 1) + (ZHI - 1) + 2)
+    pl.semaphore_wait(barrier, (nchan - 1) + (ny - 1) + (ZHI - 1) + 4)
 
     upper, lower = lax.rem(g + 1, ngrp), lax.rem(g + ngrp - 1, ngrp)
-    right, left = group_of(1), group_of(nchan - 1)
-    remote(FE.at[:, 2:3], FE.at[:, 0:1], es, er, g, right).start()
-    remote(FE.at[:, 1:2], FE.at[:, 3:4], es, er, g, left).start()
-    remote(G.at[10:11, 1:3], G.at[2:3, 1:3], ns, nr, upper, c).start()
-    remote(G.at[3:4, 1:3], G.at[11:12, 1:3], ns, nr, lower, c).start()
-    remote(G.at[8:10, 1:3], G.at[0:2, 1:3], qs, qr, upper, c).start()
-    remote(G.at[4:6, 1:3], G.at[12:14, 1:3], qs, qr, lower, c).start()
-    remote(G.at[3:11, 2:3], G.at[3:11, 0:1], rs, rr, g, right).start()
-    remote(G.at[3:11, 1:2], G.at[3:11, 3:4], rs, rr, g, left).start()
-    arrived(FE.at[:, 1:3], er)
-    for row, edge in ((0, 0), (3, nchan - 1)):
-        shifted = along_z(FE[:, row:row + 1].reshape(128, 128).astype(F32)).reshape(8, 1, 16, 384)
-        F3[:, row:row + 1] = jnp.where(c == edge, jnp.zeros_like(shifted), shifted)
-
-    feat3 = jnp.concatenate([F3[:, ty:ty + 2].reshape(256, 384) for ty in range(3)], axis=1)
-    tap_sums((1,), feat3)
-    to_partner(0)
-    arrived(G.at[0:1, 0:4], nr)
-    tap_sums((0, 2), feat3)
-    to_partner(1)
+    remote(FE.at[:, edge_row], FE.at[:, far_row], es, er, g, beyond).start()
+    remote(FE.at[:, edge_row], FE.at[:, far_row], es, er, g, facing).start()
+    remote(FE.at[:, mine], FE.at[:, mine], es, er, g, other).start()
+    remote(G.at[3:11, mine], G.at[3:11, mine], es, er, g, other).start()
+    for to in (other, c):
+        remote(G.at[10:11, mine], G.at[2:3, mine], ns, nr, upper, to).start()
+        remote(G.at[3:4, mine], G.at[11:12, mine], ns, nr, lower, to).start()
+    remote(G.at[8:10, mine], G.at[0:2, mine], qs, qr, upper, c).start()
+    remote(G.at[4:6, mine], G.at[12:14, mine], qs, qr, lower, c).start()
+    remote(G.at[3:11, edge_row], G.at[3:11, far_row], rs, rr, g, facing).start()
+    arrived(FE, er)
+    feature_rows(theirs, 2, None)
+    feature_rows(pl.ds(0, 1), 1, 0)
+    feature_rows(pl.ds(5, 1), 1, nchip - 1)
+    tiles = []
+    for n in range(5):
+        m = 4 * core + n
+        tiles.append(F3[lax.rem(m, 3), :, pl.ds(m // 3, 4)].reshape(512, 128))
+    feat3 = jnp.concatenate(tiles, axis=1)
+    tap_sums(1, feat3)
+    to_owners(0)
+    arrived(G.at[0:2, 0:4], nr)
+    tap_sums(0, feat3)
+    tap_sums(2, feat3)
+    to_owners(1)
     arrived(G.at[0:2, 0:4], qr)
-    for planes in ((0, 3), (11, 14)):
-        at = slice(planes[0], planes[1])
-        remote(G.at[at, 2:3], G.at[at, 0:1], rs, rr, g, right).start()
-        remote(G.at[at, 1:2], G.at[at, 3:4], rs, rr, g, left).start()
-    to_owners(0)
+    remote(G.at[0:3, edge_row], G.at[0:3, far_row], rs, rr, g, facing).start()
+    remote(G.at[11:14, edge_row], G.at[11:14, far_row], rs, rr, g, facing).start()
+    remote(G.at[0:2, inner_row], G.at[0:2, inner_row], rs, rr, g, other).start()
+    remote(G.at[12:14, inner_row], G.at[12:14, inner_row], rs, rr, g, other).start()
     for t in range(3):
         l_wh[t].wait()
         remote(own_rows[t], own_rows[t], ws, wr, g, other).start()
-    to_owners(1)
     l_wf.wait()
     l_up.wait()
-    sent(G.at[0:7, 0:4], rs)
-    arrived(G.at[0:7, 0:4], rr)
+    sent(G.at[0:3], rs)
+    arrived(G.at[0:3], rr)
 
     @pl.when(g == 0)
     def _():
@@ -204,17 +206,17 @@
     def _():
         G[11:14] = jnp.zeros((3,) + G.shape[1:], BF16)
 
-    @pl.when(c == 0)
+    @pl.when(chip == 0)
     def _():
         G[:, 0:1] = jnp.zeros((14, 1, 16, 128), BF16)
 
-    @pl.when(c == nchan - 1)
+    @pl.when(chip == nchip - 1)
     def _():
-        G[:, 3:4] = jnp.zeros((14, 1, 16, 128), BF16)
+        G[:, 5:6] = jnp.zeros((14, 1, 16, 128), BF16)
 
     lhs = jnp.concatenate(
         [
-            G[2 - tx:14 - tx, 2 - ty:4 - ty].reshape(384, 128)
+            G[2 - tx:14 - tx, pl.ds(2 + 2 * core - ty, 2)].reshape(384, 128)
             for tx in range(3)
             for ty in range(3)
         ],
@@ -269,11 +271,15 @@
     lax.fori_loop(1, nchan, psend, 0)
     PR[c + 1] = PS[c]
     for part in range(2):
-        arrived(SR.at[0:7, tap_rows(part)], sr.at[part])
-    total = T[core, chip]
-    for s in range(1, nchan // 2):
-        total = total + SR[lax.rem(chip + s, nchip)].astype(F32)
-    flipped = jnp.concatenate([total, jnp.zeros((32, 128), F32)], axis=0).T
+        arrived(SR.at[0:15, tap_rows(part)], sr.at[part])
+    SR[c] = SS[c]
+    sums = []
+    for k in range(2):
+        total = SR[k].astype(F32)
+        for p in range(1, nchan // 2):
+            total = total + SR[2 * p + k].astype(F32)
+        sums.append(total)
+    flipped = jnp.concatenate(sums + [jnp.zeros((32, 128), F32)], axis=0).T
     VT[...] = flipped.reshape(VT.shape)
     YS[...] = flipped.astype(BF16).reshape(YS.shape)
 
@@ -337,13 +343,12 @@
             acc = acc + FR[2 * p + k].astype(F32)
         gh_out[k * 16:(k + 1) * 16, :] = acc.astype(BF16)
 
-    sent(FE.at[:, 1:3], es)
-    sent(G.at[0:1, 0:4], ns)
+    sent(FE, es)
+    sent(G.at[0:2, 0:4], ns)
     sent(G.at[0:2, 0:4], qs)
     sent(WP.at[:, :, 0:96, :], ws)
     for part in range(2):
-        sent(XS.at[:, tap_rows(part), :], xs.at[part])
-        sent(SS.at[0:7, tap_rows(part)], ss.at[part])
+        sent(SS.at[0:15, tap_rows(part)], ss.at[part])
     sent(PS.at[0:15], ps)
     sent(FS.at[0:15], fs)
     sent(YS.at[0:7], ys)
@@ -353,16 +358,19 @@
     v3 = ZS[zh]
     for s in range(1, ZHI):
         v3 = v3 + ZR[lax.rem(zh + s, ZHI)]
-    for tx in range(3):
-        for t in range(9):
-            at = TAP_ROW[tx] + 8 * t
-            tg_out[tx * 9 + t] = v3[0:4, at:at + 8]
+    for m in range(9):
+        base = (
+            m * 8 + (40 if m < 5 else 112),
+            m * 8 if m < 5 else 112 + (m - 4) * 8,
+            (10 + m) * 8 if m < 4 else 112 + (5 + m) * 8,
+        )
+        for tx in range(3):
+            tg_out[tx * 9 + m] = v3[0:4, base[tx]:base[tx] + 8]
 
 
 def body(grad_out, feat_full, filters_full, upsample_weight, filters_half):
     nchan = lax.axis_size("chan")
     ny = lax.axis_size("grp") // ZHI
-    nchip = nchan // 2
     wide = filters_half.shape[3]
     turned = jnp.swapaxes(filters_half, 3, 4)
     V = pltpu.VMEM
@@ -378,18 +386,16 @@
         in_specs=[anyspace] * 5,
         out_specs=(vmem, vmem),
         scratch_shapes=[
-            V((14, 4, 16, 128), BF16),
-            V((8, 4, 16, 128), BF16),
-            V((8, 4, 16, 384), BF16),
+            V((14, 6, 16, 128), BF16),
+            V((8, 6, 16, 128), BF16),
+            V((3, 8, 6, 16, 128), BF16),
             V((3, 3, 3, 128, 128), BF16),
             V((2, 2, 2, wide, 128), BF16),
             V((3, 3, 256, wide), BF16),
             V((384, 128), F32),
-            V((2, nchip, 224, 128), F32),
-            V((nchip, 224, 128), BF16),
-            V((nchip, 224, 128), BF16),
-            V((nchip, 224, 128), BF16),
-            V((nchip, 224, 128), BF16),
+            V((nchan, 120, 128), F32),
+            V((nchan, 112, 128), BF16),
+            V((nchan, 112, 128), BF16),
             V((nchan, 16, 128), BF16),
             V((nchan + 2, 16, 128), BF16),
             V((3, nchan + 2, 16, 256), BF16),
@@ -402,7 +408,7 @@
             V((ZHI, 8, 256), F32),
             D((7,)),
             D, D, D, D, D, D, D, D, D, D,
-            D((2,)), D((2,)), D((2,)), D((2,)),
+            D((2,)), D((2,)),
             D, D, D, D, D, D, D, D,
         ],
         compiler_params=pltpu.CompilerParams(collective_id=0, has_side_effects=True),

time: 39.1 us -> 40.7 us (1.041)
  Pallas kernels: 37.1 us -> 38.7 us
    pallas_call x1, Pallas kernels: 37.1 us -> 38.7 us  [body(): pl.pallas_call(kernel, out_shape=(pltpu.VMEM((32, wide), BF16), pltpu.VME...]
where the time goes in v5:
time: 40.7 us; the launch traced here: 40.6 us
  Pallas kernels  38.7 us (95%)
  local copies, waits for them, and re-layouts  1.24 us (3%)
  between operations  0.64 us (2%)
    pallas_call x1, Pallas kernels, body(): pl.pallas_call(kernel, out_shape=(pltpu.VMEM((32, wide), BF16), pltpu.VME...  38.7 us
    unnamed x2, local copies, waits for them, and re-layouts  1.24 us

profile of v5, /device:TPU:1, one launch (start us, length us, event | category | flops | bytes accessed | tf_op | source)
XLA Modules:
  0.0 40.6 jit_solution(11533758816459918108)
XLA Ops:
  0.6 38.7 %shard_map.68 = (bf16[32,512]{1,0:T(8,128)(2,1)S(1)}, f32[27,4,8]{2,1,0:T(4,128)S(1)}) custom-call(bf16[8,2,16,128]{3,2,1,0:T(8,128)(2,1)} %go.1, bf16[8,2,16,128]{3,2,1,0:T(8,128)(2,1)} %fe.1, bf16[3,3,3,128,128]{4,3,2,1,0:T(8,128)(2,1)} %wf.1, bf16[2,2,2,512,128]{4,3,2,1,0:T(8,128)(2,1)} %uw.1, bf16[3,3,3,32,512]{4,3,2,1,0:T(8,128)(2,1)} %bitcast.5), custom_call_target="tpu_custom_call" | custom-call | tf_op jit(solution)/shard_map/pallas_call | solution.py:380
  39.4 0.6 %copy.9 = bf16[1,4,8,512]{3,2,1,0:T(8,128)(2,1)} copy(bf16[1,4,8,512]{3,2,1,0:T(8,128)(2,1)S(1)} %bitcast.4) | data formatting | bytes 65536
  40.0 0.6 %copy.10 = f32[3,3,3,4,8]{4,3,2,1,0:T(4,128)} copy(f32[3,3,3,4,8]{4,3,2,1,0:T(4,128)S(1)} %bitcast.3) | data formatting | bytes 6912

commit v6 on v4

--- a/solution.py
+++ b/solution.py
@@ -5,7 +5,15 @@
 from jax.experimental.pallas import tpu as pltpu
 from jax.sharding import PartitionSpec as P
 
-TAP_ROW = {1: 0, 0: 80, 2: 152}
+TAP_ROW = {
+    (tx, ty): {1: {1: 0, 0: 32, 2: 56}, 0: {0: 80, 1: 104, 2: 128}, 2: {0: 152, 1: 176, 2: 200}}[tx][ty]
+    for tx in range(3)
+    for ty in range(3)
+}
+TAP_PART = (slice(0, 32), slice(32, 80), slice(80, 224))
+FAR_CHIPS = ((1, 2), (0, 2), (1, 1), (1, 3), (0, 1), (0, 3), (1, 0))
+FAR_Y = (4, 3, 5, 2, 6, 1, 7)
+FAR_Z = (2, 1, 3)
 F32 = jnp.float32
 BF16 = jnp.bfloat16
 MESH = pl.DeviceIdType.MESH
@@ -62,10 +70,13 @@
         d = lax.rem(y + s, ny)
         return remote(YS.at[d], YR.at[y], ys, yr, d * ZHI + zh, c)
 
-    def tap_rows(part):
-        return slice(0, 80) if part == 0 else slice(80, 224)
-
-    def tap_sums(txs, feat3):
+    def chip_at(dz, dx):
+        return (chip // 4 + dz) % 2 * 4 + (chip % 4 + dx) % 4
+
+    far_chips = [chip_at(dz, dx) for dz, dx in FAR_CHIPS]
+    far_members = [2 * p + k for p in far_chips for k in range(2)] + [other]
+
+    def tap_sums(txs, tys, feat3):
         planes = []
         for tx in txs:
             if tx == 0:
@@ -81,32 +92,32 @@
             jnp.concatenate(planes, axis=1), feat3, TN, preferred_element_type=F32
         )
         for n, tx in enumerate(txs):
-            rows = part[n * 128:(n + 1) * 128].reshape(nchip, 2, 8, 9 * 128)
-            for t in range(9):
-                at = TAP_ROW[tx] + t * 8
-                for k in range(2):
-                    T[k, :, at:at + 8, :] = rows[:, k, :, t * 128:(t + 1) * 128]
+            rows = part[n * 128:(n + 1) * 128].reshape(nchip, 2, 8, feat3.shape[1])
+            for m, ty in enumerate(tys):
+                for tz in range(3):
+                    at = TAP_ROW[tx, ty] + tz * 8
+                    t = (m * 3 + tz) * 128
+                    for k in range(2):
+                        T[k, :, at:at + 8, :] = rows[:, k, :, t:t + 128]
 
     def to_partner(part):
-        rows = tap_rows(part)
+        rows = TAP_PART[part]
         XS[:, rows, :] = T[1 - core, :, rows, :].astype(BF16)
         remote(XS.at[:, rows, :], XR.at[:, rows, :], xs.at[part], xr.at[part], g, other).start()
 
     def to_owners(part):
-        rows = tap_rows(part)
+        rows = TAP_PART[part]
         arrived(XR.at[:, rows, :], xr.at[part])
         summed = T[core, :, rows, :] + XR[:, rows, :].astype(F32)
         T[core, :, rows, :] = summed
         SS[:, rows, :] = summed.astype(BF16)
-
-        def ssend(s, _):
-            d = lax.rem(chip + s, nchip)
+        for d in far_chips:
             remote(
                 SS.at[d, rows], SR.at[chip, rows], ss.at[part], sr.at[part], g, 2 * d + core
             ).start()
-            return 0
-
-        lax.fori_loop(1, nchip, ssend, 0)
+
+    def feat_rows(tys):
+        return jnp.concatenate([F3[:, ty:ty + 2].reshape(256, 384) for ty in tys], axis=1)
 
     def along_z(cells):
         z_of = lax.broadcasted_iota(jnp.int32, cells.shape, 0) % 16
@@ -153,10 +164,11 @@
     PR[0] = jnp.zeros(PR.shape[1:], BF16)
     PR[nchan + 1] = jnp.zeros(PR.shape[1:], BF16)
     WP[:, :, 192:256, :] = jnp.zeros((3, 3, 64, WP.shape[3]), BF16)
-    T[:, :, 72:80, :] = jnp.zeros((2, nchip, 8, 128), F32)
+    T[:, :, 24:32, :] = jnp.zeros((2, nchip, 8, 128), F32)
     l_fe.wait()
     F3[:, 1:3] = along_z(FE[:, 1:3].reshape(256, 128).astype(F32)).reshape(8, 2, 16, 384)
     l_go.wait()
+    tap_sums((1,), (1,), feat_rows((1,)))
 
     pl.semaphore_wait(barrier, (nchan - 1) + (ny - 1) + (ZHI - 1) + 2)
 
@@ -170,27 +182,28 @@
     remote(G.at[4:6, 1:3], G.at[12:14, 1:3], qs, qr, lower, c).start()
     remote(G.at[3:11, 2:3], G.at[3:11, 0:1], rs, rr, g, right).start()
     remote(G.at[3:11, 1:2], G.at[3:11, 3:4], rs, rr, g, left).start()
+    to_partner(0)
+    to_owners(0)
     arrived(FE.at[:, 1:3], er)
     for row, edge in ((0, 0), (3, nchan - 1)):
         shifted = along_z(FE[:, row:row + 1].reshape(128, 128).astype(F32)).reshape(8, 1, 16, 384)
         F3[:, row:row + 1] = jnp.where(c == edge, jnp.zeros_like(shifted), shifted)
 
-    feat3 = jnp.concatenate([F3[:, ty:ty + 2].reshape(256, 384) for ty in range(3)], axis=1)
-    tap_sums((1,), feat3)
-    to_partner(0)
+    tap_sums((1,), (0, 2), feat_rows((0, 2)))
+    to_partner(1)
     arrived(G.at[0:1, 0:4], nr)
-    tap_sums((0, 2), feat3)
-    to_partner(1)
+    tap_sums((0, 2), (0, 1, 2), feat_rows((0, 1, 2)))
+    to_partner(2)
     arrived(G.at[0:2, 0:4], qr)
     for planes in ((0, 3), (11, 14)):
         at = slice(planes[0], planes[1])
         remote(G.at[at, 2:3], G.at[at, 0:1], rs, rr, g, right).start()
         remote(G.at[at, 1:2], G.at[at, 3:4], rs, rr, g, left).start()
-    to_owners(0)
+    to_owners(1)
     for t in range(3):
         l_wh[t].wait()
         remote(own_rows[t], own_rows[t], ws, wr, g, other).start()
-    to_owners(1)
+    to_owners(2)
     l_wf.wait()
     l_up.wait()
     sent(G.at[0:7, 0:4], rs)
@@ -261,15 +274,11 @@
                 ]
                 PS[2 * d + k] = jnp.concatenate(pair, axis=0).astype(BF16)
 
-    def psend(s, _):
-        d = group_of(s)
+    for d in far_members:
         remote(PS.at[d], PR.at[c + 1], ps, pr, g, d).start()
-        return 0
-
-    lax.fori_loop(1, nchan, psend, 0)
     PR[c + 1] = PS[c]
-    for part in range(2):
-        arrived(SR.at[0:7, tap_rows(part)], sr.at[part])
+    for part in range(3):
+        arrived(SR.at[0:7, TAP_PART[part]], sr.at[part])
     total = T[core, chip]
     for s in range(1, nchan // 2):
         total = total + SR[lax.rem(chip + s, nchip)].astype(F32)
@@ -277,11 +286,8 @@
     VT[...] = flipped.reshape(VT.shape)
     YS[...] = flipped.astype(BF16).reshape(YS.shape)
 
-    def ysend(s, _):
+    for s in FAR_Y:
         ycopy(s).start()
-        return 0
-
-    lax.fori_loop(1, ny, ysend, 0)
 
     arrived(WP.at[:, :, 0:96, :], wr)
     arrived(PR.at[0:15], pr)
@@ -308,12 +314,8 @@
     part = jnp.dot(lhs, WP[...].reshape(9 * 256, 512), preferred_element_type=F32)
     FS[...] = part.astype(BF16).reshape(FS.shape)
 
-    def fsend(s, _):
-        d = group_of(s)
+    for d in far_members:
         remote(FS.at[d], FR.at[c], fs, fr, g, d).start()
-        return 0
-
-    lax.fori_loop(1, nchan, fsend, 0)
     FR[c] = FS[c]
 
     arrived(YR.at[0:7], yr)
@@ -321,14 +323,11 @@
     for s in range(1, YR.shape[0]):
         v2 = v2 + YR[lax.rem(y + s, ny)].astype(F32)
     for q in range(ZHI):
-        ZS[q] = jnp.concatenate([v2[4 * q:4 * q + 4], jnp.zeros((4, 256), F32)], axis=0)
-
-    def zsend(s, _):
+        rows = v2[4 * q:4 * q + 4]
+        ZS[q] = jnp.concatenate([rows[:, 0:128], rows[:, 128:256]], axis=0)
+    for s in FAR_Z:
         d = lax.rem(zh + s, ZHI)
         remote(ZS.at[d], ZR.at[zh], zs, zr, y * ZHI + d, c).start()
-        return 0
-
-    lax.fori_loop(1, ZHI, zsend, 0)
 
     arrived(FR.at[0:15], fr)
     for k in range(2):
@@ -341,9 +340,9 @@
     sent(G.at[0:1, 0:4], ns)
     sent(G.at[0:2, 0:4], qs)
     sent(WP.at[:, :, 0:96, :], ws)
-    for part in range(2):
-        sent(XS.at[:, tap_rows(part), :], xs.at[part])
-        sent(SS.at[0:7, tap_rows(part)], ss.at[part])
+    for part in range(3):
+        sent(XS.at[:, TAP_PART[part], :], xs.at[part])
+        sent(SS.at[0:7, TAP_PART[part]], ss.at[part])
     sent(PS.at[0:15], ps)
     sent(FS.at[0:15], fs)
     sent(YS.at[0:7], ys)
@@ -354,9 +353,11 @@
     for s in range(1, ZHI):
         v3 = v3 + ZR[lax.rem(zh + s, ZHI)]
     for tx in range(3):
-        for t in range(9):
-            at = TAP_ROW[tx] + 8 * t
-            tg_out[tx * 9 + t] = v3[0:4, at:at + 8]
+        for ty in range(3):
+            for tz in range(3):
+                at = TAP_ROW[tx, ty] + tz * 8
+                row, lane = at // 128 * 4, at % 128
+                tg_out[(tx * 3 + ty) * 3 + tz] = v3[row:row + 4, lane:lane + 8]
 
 
 def body(grad_out, feat_full, filters_full, upsample_weight, filters_half):
@@ -398,11 +399,11 @@
             V((ny, 16, 256), F32),
             V((ny, 16, 256), BF16),
             V((ny, 16, 256), BF16),
-            V((ZHI, 8, 256), F32),
-            V((ZHI, 8, 256), F32),
+            V((ZHI, 8, 128), F32),
+            V((ZHI, 8, 128), F32),
             D((7,)),
             D, D, D, D, D, D, D, D, D, D,
-            D((2,)), D((2,)), D((2,)), D((2,)),
+            D((3,)), D((3,)), D((3,)), D((3,)),
             D, D, D, D, D, D, D, D,
         ],
         compiler_params=pltpu.CompilerParams(collective_id=0, has_side_effects=True),

time: 39.1 us -> 37.6 us (0.962)
  Pallas kernels: 37.1 us -> 35.6 us
    pallas_call x1, Pallas kernels: 37.1 us -> 35.6 us  [body(): pl.pallas_call(kernel, out_shape=(pltpu.VMEM((32, wide), BF16), pltpu.VME...]
where the time goes in v6:
time: 37.6 us; the launch traced here: 37.4 us
  Pallas kernels  35.6 us (95%)
  local copies, waits for them, and re-layouts  1.24 us (3%)
  between operations  0.64 us (2%)
    pallas_call x1, Pallas kernels, body(): pl.pallas_call(kernel, out_shape=(pltpu.VMEM((32, wide), BF16), pltpu.VME...  35.6 us
    unnamed x2, local copies, waits for them, and re-layouts  1.24 us

profile of v6, /device:TPU:1, one launch (start us, length us, event | category | flops | bytes accessed | tf_op | source)
XLA Modules:
  0.0 37.4 jit_solution(15108854255690097761)
XLA Ops:
  0.6 35.6 %shard_map.68 = (bf16[32,512]{1,0:T(8,128)(2,1)S(1)}, f32[27,4,8]{2,1,0:T(4,128)S(1)}) custom-call(bf16[8,2,16,128]{3,2,1,0:T(8,128)(2,1)} %go.1, bf16[8,2,16,128]{3,2,1,0:T(8,128)(2,1)} %fe.1, bf16[3,3,3,128,128]{4,3,2,1,0:T(8,128)(2,1)} %wf.1, bf16[2,2,2,512,128]{4,3,2,1,0:T(8,128)(2,1)} %uw.1, bf16[3,3,3,32,512]{4,3,2,1,0:T(8,128)(2,1)} %bitcast.5), custom_call_target="tpu_custom_call" | custom-call | tf_op jit(solution)/shard_map/pallas_call | solution.py:373
  36.2 0.6 %copy.9 = bf16[1,4,8,512]{3,2,1,0:T(8,128)(2,1)} copy(bf16[1,4,8,512]{3,2,1,0:T(8,128)(2,1)S(1)} %bitcast.4) | data formatting | bytes 65536
  36.8 0.6 %copy.10 = f32[3,3,3,4,8]{4,3,2,1,0:T(4,128)} copy(f32[3,3,3,4,8]{4,3,2,1,0:T(4,128)S(1)} %bitcast.3) | data formatting | bytes 6912

commit v7 on v6

--- a/solution.py
+++ b/solution.py
@@ -5,6 +5,7 @@
 from jax.experimental.pallas import tpu as pltpu
 from jax.sharding import PartitionSpec as P
 
+ZHI = 4
 TAP_ROW = {
     (tx, ty): {1: {1: 0, 0: 32, 2: 56}, 0: {0: 80, 1: 104, 2: 128}, 2: {0: 152, 1: 176, 2: 200}}[tx][ty]
     for tx in range(3)
@@ -12,14 +13,15 @@
 }
 TAP_PART = (slice(0, 32), slice(32, 80), slice(80, 224))
 FAR_CHIPS = ((1, 2), (0, 2), (1, 1), (1, 3), (0, 1), (0, 3), (1, 0))
-FAR_Y = (4, 3, 5, 2, 6, 1, 7)
-FAR_Z = (2, 1, 3)
+FAR_GROUPS = sorted(
+    ((dy, dz) for dy in range(8) for dz in range(ZHI) if dy + dz > 0),
+    key=lambda d: -(min(d[0], 8 - d[0]) + 2 * min(d[1], ZHI - d[1])),
+)
 F32 = jnp.float32
 BF16 = jnp.bfloat16
 MESH = pl.DeviceIdType.MESH
 NT = (((1,), (1,)), ((), ()))
 TN = (((0,), (0,)), ((), ()))
-ZHI = 4
 
 
 def kernel(
@@ -28,8 +30,8 @@
     G, FE, F3, WF, UP, WP, IG,
     T, XS, XR, SS, SR,
     PS, PR, SA, FS, FR,
-    VT, YS, YR, ZS, ZR,
-    lsem, es, er, ns, nr, qs, qr, rs, rr, ws, wr, xs, xr, ss, sr, ps, pr, fs, fr, ys, yr, zs, zr,
+    YS, YR,
+    lsem, es, er, ns, nr, qs, qr, rs, rr, ws, wr, xs, xr, ss, sr, ps, pr, fs, fr, ys, yr, ready,
 ):
     g = lax.axis_index("grp")
     c = lax.axis_index("chan")
@@ -65,10 +67,6 @@
 
     def arrived(ref, sem):
         remote(ref, ref, sem, sem, g, other).wait_recv()
-
-    def ycopy(s):
-        d = lax.rem(y + s, ny)
-        return remote(YS.at[d], YR.at[y], ys, yr, d * ZHI + zh, c)
 
     def chip_at(dz, dx):
         return (chip // 4 + dz) % 2 * 4 + (chip % 4 + dx) % 4
@@ -182,6 +180,8 @@
     remote(G.at[4:6, 1:3], G.at[12:14, 1:3], qs, qr, lower, c).start()
     remote(G.at[3:11, 2:3], G.at[3:11, 0:1], rs, rr, g, right).start()
     remote(G.at[3:11, 1:2], G.at[3:11, 3:4], rs, rr, g, left).start()
+    for s in range(1, ZHI):
+        pl.semaphore_signal(ready, inc=1, device_id=dev(zgrp(s), c), device_id_type=MESH)
     to_partner(0)
     to_owners(0)
     arrived(FE.at[:, 1:3], er)
@@ -277,17 +277,24 @@
     for d in far_members:
         remote(PS.at[d], PR.at[c + 1], ps, pr, g, d).start()
     PR[c + 1] = PS[c]
+    sums = []
     for part in range(3):
         arrived(SR.at[0:7, TAP_PART[part]], sr.at[part])
-    total = T[core, chip]
-    for s in range(1, nchan // 2):
-        total = total + SR[lax.rem(chip + s, nchip)].astype(F32)
-    flipped = jnp.concatenate([total, jnp.zeros((32, 128), F32)], axis=0).T
-    VT[...] = flipped.reshape(VT.shape)
-    YS[...] = flipped.astype(BF16).reshape(YS.shape)
-
-    for s in FAR_Y:
-        ycopy(s).start()
+        total = T[core, chip, TAP_PART[part], :]
+        for s in range(1, nchan // 2):
+            total = total + SR[lax.rem(chip + s, nchip), TAP_PART[part], :].astype(F32)
+        sums.append(total)
+    flipped = jnp.concatenate(sums + [jnp.zeros((32, 128), F32)], axis=0).T
+    top = lax.broadcasted_iota(jnp.int32, (8, 128), 0) < 4
+    for r in range(16):
+        left_half, right_half = flipped[8 * r:8 * r + 8, 0:128], flipped[8 * r:8 * r + 8, 128:256]
+        YS[2 * r] = jnp.where(top, left_half, pltpu.roll(right_half, 4, 0)).astype(BF16)
+        YS[2 * r + 1] = jnp.where(top, pltpu.roll(left_half, 4, 0), right_half).astype(BF16)
+    pl.semaphore_wait(ready, ZHI - 1)
+    for dy, dz in FAR_GROUPS:
+        to = lax.rem(y + dy, ny) * ZHI + lax.rem(zh + dz, ZHI)
+        remote(YS.at[to], YR.at[g], ys, yr, to, c).start()
+    YR[g] = YS[g]
 
     arrived(WP.at[:, :, 0:96, :], wr)
     arrived(PR.at[0:15], pr)
@@ -318,17 +325,6 @@
         remote(FS.at[d], FR.at[c], fs, fr, g, d).start()
     FR[c] = FS[c]
 
-    arrived(YR.at[0:7], yr)
-    v2 = VT[y]
-    for s in range(1, YR.shape[0]):
-        v2 = v2 + YR[lax.rem(y + s, ny)].astype(F32)
-    for q in range(ZHI):
-        rows = v2[4 * q:4 * q + 4]
-        ZS[q] = jnp.concatenate([rows[:, 0:128], rows[:, 128:256]], axis=0)
-    for s in FAR_Z:
-        d = lax.rem(zh + s, ZHI)
-        remote(ZS.at[d], ZR.at[zh], zs, zr, y * ZHI + d, c).start()
-
     arrived(FR.at[0:15], fr)
     for k in range(2):
         acc = FR[k].astype(F32)
@@ -345,13 +341,12 @@
         sent(SS.at[0:7, TAP_PART[part]], ss.at[part])
     sent(PS.at[0:15], ps)
     sent(FS.at[0:15], fs)
-    sent(YS.at[0:7], ys)
-    sent(ZS.at[0:3], zs)
-
-    arrived(ZR.at[0:3], zr)
-    v3 = ZS[zh]
-    for s in range(1, ZHI):
-        v3 = v3 + ZR[lax.rem(zh + s, ZHI)]
+    sent(YS.at[0:31], ys)
+
+    arrived(YR.at[0:31], yr)
+    v3 = YR[0].astype(F32)
+    for o in range(1, 32):
+        v3 = v3 + YR[o].astype(F32)
     for tx in range(3):
         for ty in range(3):
             for tz in range(3):
@@ -362,7 +357,6 @@
 
 def body(grad_out, feat_full, filters_full, upsample_weight, filters_half):
     nchan = lax.axis_size("chan")
-    ny = lax.axis_size("grp") // ZHI
     nchip = nchan // 2
     wide = filters_half.shape[3]
     turned = jnp.swapaxes(filters_half, 3, 4)
@@ -396,15 +390,12 @@
             V((3, nchan + 2, 16, 256), BF16),
             V((nchan, 16, wide), BF16),
             V((nchan, 16, wide), BF16),
-            V((ny, 16, 256), F32),
-            V((ny, 16, 256), BF16),
-            V((ny, 16, 256), BF16),
-            V((ZHI, 8, 128), F32),
-            V((ZHI, 8, 128), F32),
+            V((32, 8, 128), BF16),
+            V((32, 8, 128), BF16),
             D((7,)),
             D, D, D, D, D, D, D, D, D, D,
             D((3,)), D((3,)), D((3,)), D((3,)),
-            D, D, D, D, D, D, D, D,
+            D, D, D, D, D, D, pltpu.SemaphoreType.REGULAR,
         ],
         compiler_params=pltpu.CompilerParams(collective_id=0, has_side_effects=True),
     )(grad_out, feat_full, filters_full, upsample_weight, turned)

time: 37.6 us -> 37.1 us (0.987)
  Pallas kernels: 35.6 us -> 35 us
    pallas_call x1, Pallas kernels: 35.6 us -> 35 us  [body(): pl.pallas_call(kernel, out_shape=(pltpu.VMEM((32, wide), BF16), pltpu.VME...]
where the time goes in v7:
time: 37.1 us; the launch traced here: 36.9 us
  Pallas kernels  35 us (94%)
  local copies, waits for them, and re-layouts  1.24 us (3%)
  between operations  0.64 us (2%)
    pallas_call x1, Pallas kernels, body(): pl.pallas_call(kernel, out_shape=(pltpu.VMEM((32, wide), BF16), pltpu.VME...  35 us
    unnamed x2, local copies, waits for them, and re-layouts  1.24 us

profile of v7, /device:TPU:1, one launch (start us, length us, event | category | flops | bytes accessed | tf_op | source)
XLA Modules:
  0.0 36.9 jit_solution(5550840532319024012)
XLA Ops:
  0.6 35.0 %shard_map.68 = (bf16[32,512]{1,0:T(8,128)(2,1)S(1)}, f32[27,4,8]{2,1,0:T(4,128)S(1)}) custom-call(bf16[8,2,16,128]{3,2,1,0:T(8,128)(2,1)} %go.1, bf16[8,2,16,128]{3,2,1,0:T(8,128)(2,1)} %fe.1, bf16[3,3,3,128,128]{4,3,2,1,0:T(8,128)(2,1)} %wf.1, bf16[2,2,2,512,128]{4,3,2,1,0:T(8,128)(2,1)} %uw.1, bf16[3,3,3,32,512]{4,3,2,1,0:T(8,128)(2,1)} %bitcast.5), custom_call_target="tpu_custom_call" | custom-call | tf_op jit(solution)/shard_map/pallas_call | solution.py:367
  35.7 0.6 %copy.9 = bf16[1,4,8,512]{3,2,1,0:T(8,128)(2,1)} copy(bf16[1,4,8,512]{3,2,1,0:T(8,128)(2,1)S(1)} %bitcast.4) | data formatting | bytes 65536
  36.3 0.6 %copy.10 = f32[3,3,3,4,8]{4,3,2,1,0:T(4,128)} copy(f32[3,3,3,4,8]{4,3,2,1,0:T(4,128)S(1)} %bitcast.3) | data formatting | bytes 6912

commit v8 on v7

--- a/solution.py
+++ b/solution.py
@@ -31,7 +31,7 @@
     T, XS, XR, SS, SR,
     PS, PR, SA, FS, FR,
     YS, YR,
-    lsem, es, er, ns, nr, qs, qr, rs, rr, ws, wr, xs, xr, ss, sr, ps, pr, fs, fr, ys, yr, ready,
+    lsem, es, er, ns, nr, qs, qr, bs, br, rs, rr, ws, wr, xs, xr, ss, sr, ps, pr, fs, fr, ys, yr, ready,
 ):
     g = lax.axis_index("grp")
     c = lax.axis_index("chan")
@@ -178,8 +178,8 @@
     remote(G.at[3:4, 1:3], G.at[11:12, 1:3], ns, nr, lower, c).start()
     remote(G.at[8:10, 1:3], G.at[0:2, 1:3], qs, qr, upper, c).start()
     remote(G.at[4:6, 1:3], G.at[12:14, 1:3], qs, qr, lower, c).start()
-    remote(G.at[3:11, 2:3], G.at[3:11, 0:1], rs, rr, g, right).start()
-    remote(G.at[3:11, 1:2], G.at[3:11, 3:4], rs, rr, g, left).start()
+    remote(G.at[3:11, 2:3], G.at[3:11, 0:1], bs, br, g, right).start()
+    remote(G.at[3:11, 1:2], G.at[3:11, 3:4], bs, br, g, left).start()
     for s in range(1, ZHI):
         pl.semaphore_signal(ready, inc=1, device_id=dev(zgrp(s), c), device_id_type=MESH)
     to_partner(0)
@@ -192,13 +192,13 @@
     tap_sums((1,), (0, 2), feat_rows((0, 2)))
     to_partner(1)
     arrived(G.at[0:1, 0:4], nr)
-    tap_sums((0, 2), (0, 1, 2), feat_rows((0, 1, 2)))
-    to_partner(2)
     arrived(G.at[0:2, 0:4], qr)
     for planes in ((0, 3), (11, 14)):
         at = slice(planes[0], planes[1])
         remote(G.at[at, 2:3], G.at[at, 0:1], rs, rr, g, right).start()
         remote(G.at[at, 1:2], G.at[at, 3:4], rs, rr, g, left).start()
+    tap_sums((0, 2), (0, 1, 2), feat_rows((0, 1, 2)))
+    to_partner(2)
     to_owners(1)
     for t in range(3):
         l_wh[t].wait()
@@ -206,8 +206,42 @@
     to_owners(2)
     l_wf.wait()
     l_up.wait()
-    sent(G.at[0:7, 0:4], rs)
-    arrived(G.at[0:7, 0:4], rr)
+    arrived(G.at[0:4, 0:4], br)
+
+    @pl.when(c == 0)
+    def _():
+        G[3:11, 0:1] = jnp.zeros((8, 1, 16, 128), BF16)
+
+    @pl.when(c == nchan - 1)
+    def _():
+        G[3:11, 3:4] = jnp.zeros((8, 1, 16, 128), BF16)
+
+    def gradient(starts, count, places):
+        lhs = jnp.concatenate(
+            [
+                jnp.concatenate(
+                    [G[s - tx:s - tx + count, 2 - ty:4 - ty].reshape(count * 32, 128) for s in starts],
+                    axis=0,
+                )
+                for tx in range(3)
+                for ty in range(3)
+            ],
+            axis=1,
+        )
+        rhs = jnp.concatenate(
+            [WF[tx, ty].reshape(384, 128) for tx in range(3) for ty in range(3)], axis=1
+        )
+        grown = lax.dot_general(lhs, rhs, NT, preferred_element_type=F32)
+        z_at = lax.broadcasted_iota(jnp.int32, (192, 128), 0) % 16
+        up = jnp.where(z_at < 15, pltpu.roll(grown[:, 0:128], 191, 0), 0.0)
+        down = jnp.where(z_at > 0, pltpu.roll(grown[:, 256:384], 1, 0), 0.0)
+        whole = grown[:, 128:256] + up + down
+        for n, place in enumerate(places):
+            IG[place:place + count * 32, :] = whole[n * count * 32:(n + 1) * count * 32]
+
+    gradient((5,), 6, (96,))
+    sent(G.at[0:3, 0:4], rs)
+    arrived(G.at[0:3, 0:4], rr)
 
     @pl.when(g == 0)
     def _():
@@ -225,22 +259,7 @@
     def _():
         G[:, 3:4] = jnp.zeros((14, 1, 16, 128), BF16)
 
-    lhs = jnp.concatenate(
-        [
-            G[2 - tx:14 - tx, 2 - ty:4 - ty].reshape(384, 128)
-            for tx in range(3)
-            for ty in range(3)
-        ],
-        axis=1,
-    )
-    rhs = jnp.concatenate(
-        [WF[tx, ty].reshape(384, 128) for tx in range(3) for ty in range(3)], axis=1
-    )
-    grown = lax.dot_general(lhs, rhs, NT, preferred_element_type=F32)
-    z_at = lax.broadcasted_iota(jnp.int32, (384, 128), 0) % 16
-    up = jnp.where(z_at < 15, pltpu.roll(grown[:, 0:128], 383, 0), 0.0)
-    down = jnp.where(z_at > 0, pltpu.roll(grown[:, 256:384], 1, 0), 0.0)
-    IG[...] = grown[:, 128:256] + up + down
+    gradient((2, 11), 3, (0, 288))
 
     coarse = jnp.zeros((48, 512), F32)
     for a in range(2):
@@ -318,11 +337,12 @@
         ],
         axis=1,
     )
-    part = jnp.dot(lhs, WP[...].reshape(9 * 256, 512), preferred_element_type=F32)
-    FS[...] = part.astype(BF16).reshape(FS.shape)
-
-    for d in far_members:
-        remote(FS.at[d], FR.at[c], fs, fr, g, d).start()
+    for half in range(2):
+        cols = slice(half * 256, half * 256 + 256)
+        part = jnp.dot(lhs, WP[:, :, :, cols].reshape(9 * 256, 256), preferred_element_type=F32)
+        FS[:, :, cols] = part.astype(BF16).reshape(nchan, 16, 256)
+        for d in far_members:
+            remote(FS.at[d, :, cols], FR.at[c, :, cols], fs, fr, g, d).start()
     FR[c] = FS[c]
 
     arrived(FR.at[0:15], fr)
@@ -335,6 +355,7 @@
     sent(FE.at[:, 1:3], es)
     sent(G.at[0:1, 0:4], ns)
     sent(G.at[0:2, 0:4], qs)
+    sent(G.at[0:4, 0:4], bs)
     sent(WP.at[:, :, 0:96, :], ws)
     for part in range(3):
         sent(XS.at[:, TAP_PART[part], :], xs.at[part])
@@ -393,7 +414,7 @@
             V((32, 8, 128), BF16),
             V((32, 8, 128), BF16),
             D((7,)),
-            D, D, D, D, D, D, D, D, D, D,
+            D, D, D, D, D, D, D, D, D, D, D, D,
             D((3,)), D((3,)), D((3,)), D((3,)),
             D, D, D, D, D, D, pltpu.SemaphoreType.REGULAR,
         ],

time: 37.1 us -> 37.5 us (1.011)
  Pallas kernels: 35 us -> 35.5 us
    pallas_call x1, Pallas kernels: 35 us -> 35.5 us  [body(): pl.pallas_call(kernel, out_shape=(pltpu.VMEM((32, wide), BF16), pltpu.VME...]
where the time goes in v8:
time: 37.5 us; the launch traced here: 37.4 us
  Pallas kernels  35.5 us (95%)
  local copies, waits for them, and re-layouts  1.24 us (3%)
  between operations  0.64 us (2%)
    pallas_call x1, Pallas kernels, body(): pl.pallas_call(kernel, out_shape=(pltpu.VMEM((32, wide), BF16), pltpu.VME...  35.5 us
    unnamed x2, local copies, waits for them, and re-layouts  1.24 us

profile of v8, /device:TPU:1, one launch (start us, length us, event | category | flops | bytes accessed | tf_op | source)
XLA Modules:
  0.0 37.4 jit_solution(6076543500318010438)
XLA Ops:
  0.6 35.5 %shard_map.68 = (bf16[32,512]{1,0:T(8,128)(2,1)S(1)}, f32[27,4,8]{2,1,0:T(4,128)S(1)}) custom-call(bf16[8,2,16,128]{3,2,1,0:T(8,128)(2,1)} %go.1, bf16[8,2,16,128]{3,2,1,0:T(8,128)(2,1)} %fe.1, bf16[3,3,3,128,128]{4,3,2,1,0:T(8,128)(2,1)} %wf.1, bf16[2,2,2,512,128]{4,3,2,1,0:T(8,128)(2,1)} %uw.1, bf16[3,3,3,32,512]{4,3,2,1,0:T(8,128)(2,1)} %bitcast.5), custom_call_target="tpu_custom_call" | custom-call | tf_op jit(solution)/shard_map/pallas_call | solution.py:388
  36.1 0.6 %copy.9 = bf16[1,4,8,512]{3,2,1,0:T(8,128)(2,1)} copy(bf16[1,4,8,512]{3,2,1,0:T(8,128)(2,1)S(1)} %bitcast.4) | data formatting | bytes 65536
  36.8 0.6 %copy.10 = f32[3,3,3,4,8]{4,3,2,1,0:T(4,128)} copy(f32[3,3,3,4,8]{4,3,2,1,0:T(4,128)S(1)} %bitcast.3) | data formatting | bytes 6912

commit v9 on v8

--- a/solution.py
+++ b/solution.py
@@ -72,7 +72,10 @@
         return (chip // 4 + dz) % 2 * 4 + (chip % 4 + dx) % 4
 
     far_chips = [chip_at(dz, dx) for dz, dx in FAR_CHIPS]
-    far_members = [2 * p + k for p in far_chips for k in range(2)] + [other]
+    far_members = [
+        (2 * p + k, dz) for p, (dz, _) in zip(far_chips, FAR_CHIPS) for k in range(2)
+    ] + [(other, 0)]
+    near_side, far_side = c // 8 * 8, 8 - c // 8 * 8
 
     def tap_sums(txs, tys, feat3):
         planes = []
@@ -159,8 +162,8 @@
     lax.fori_loop(1, ZHI, hello_z, 0)
     lax.fori_loop(1, nchan, hello_group, 0)
 
-    PR[0] = jnp.zeros(PR.shape[1:], BF16)
-    PR[nchan + 1] = jnp.zeros(PR.shape[1:], BF16)
+    for slot in (0, nchan + 1):
+        SA[:, slot] = jnp.zeros((3, 16, 256), BF16)
     WP[:, :, 192:256, :] = jnp.zeros((3, 3, 64, WP.shape[3]), BF16)
     T[:, :, 24:32, :] = jnp.zeros((2, nchip, 8, 128), F32)
     l_fe.wait()
@@ -293,8 +296,8 @@
                 ]
                 PS[2 * d + k] = jnp.concatenate(pair, axis=0).astype(BF16)
 
-    for d in far_members:
-        remote(PS.at[d], PR.at[c + 1], ps, pr, g, d).start()
+    for d, dz in far_members:
+        remote(PS.at[d], PR.at[c + 1], ps, pr.at[dz], g, d).start()
     PR[c + 1] = PS[c]
     sums = []
     for part in range(3):
@@ -316,19 +319,20 @@
     YR[g] = YS[g]
 
     arrived(WP.at[:, :, 0:96, :], wr)
-    arrived(PR.at[0:15], pr)
-    rows = (nchan + 2) * 8
-    slab = PR[...].astype(F32)
-    slab = jnp.concatenate([slab[:, 0:8, :], slab[:, 8:16, :]], axis=2).reshape(rows, 256)
-    k_of = lax.broadcasted_iota(jnp.int32, (rows, 256), 0) % 8
-    shifted = (
-        jnp.where(k_of < 7, pltpu.roll(slab, rows - 1, 0), 0.0),
-        slab,
-        jnp.where(k_of > 0, pltpu.roll(slab, 1, 0), 0.0),
-    )
-    for tz in range(3):
-        pair = [v.reshape(nchan + 2, 8, 256) for v in (shifted[tz], pltpu.roll(shifted[tz], 192, 1))]
-        SA[tz] = jnp.concatenate(pair, axis=1).astype(BF16)
+    k_of = lax.broadcasted_iota(jnp.int32, (64, 256), 0) % 8
+    for dz, count, side in ((0, 7, near_side), (1, 8, far_side)):
+        arrived(PR.at[0:count], pr.at[dz])
+        slots = pl.ds(1 + side, 8)
+        slab = PR[slots].astype(F32)
+        slab = jnp.concatenate([slab[:, 0:8, :], slab[:, 8:16, :]], axis=2).reshape(64, 256)
+        shifted = (
+            jnp.where(k_of < 7, pltpu.roll(slab, 63, 0), 0.0),
+            slab,
+            jnp.where(k_of > 0, pltpu.roll(slab, 1, 0), 0.0),
+        )
+        for tz in range(3):
+            pair = [v.reshape(8, 8, 256) for v in (shifted[tz], pltpu.roll(shifted[tz], 192, 1))]
+            SA[tz, slots] = jnp.concatenate(pair, axis=1).astype(BF16)
     lhs = jnp.concatenate(
         [
             SA[tz, 2 - ty:2 - ty + nchan].reshape(nchan * 16, 256)
@@ -337,20 +341,20 @@
         ],
         axis=1,
     )
-    for half in range(2):
-        cols = slice(half * 256, half * 256 + 256)
-        part = jnp.dot(lhs, WP[:, :, :, cols].reshape(9 * 256, 256), preferred_element_type=F32)
-        FS[:, :, cols] = part.astype(BF16).reshape(nchan, 16, 256)
-        for d in far_members:
-            remote(FS.at[d, :, cols], FR.at[c, :, cols], fs, fr, g, d).start()
+    part = jnp.dot(lhs, WP[...].reshape(9 * 256, 512), preferred_element_type=F32)
+    FS[...] = part.astype(BF16).reshape(FS.shape)
+    for d, dz in far_members:
+        remote(FS.at[d], FR.at[c], fs, fr.at[dz], g, d).start()
     FR[c] = FS[c]
 
-    arrived(FR.at[0:15], fr)
+    half_sums = [jnp.zeros((16, FR.shape[2]), F32)] * 2
+    for dz, count, side in ((0, 7, near_side), (1, 8, far_side)):
+        arrived(FR.at[0:count], fr.at[dz])
+        for k in range(2):
+            for p in range(4):
+                half_sums[k] = half_sums[k] + FR[side + 2 * p + k].astype(F32)
     for k in range(2):
-        acc = FR[k].astype(F32)
-        for p in range(1, nchan // 2):
-            acc = acc + FR[2 * p + k].astype(F32)
-        gh_out[k * 16:(k + 1) * 16, :] = acc.astype(BF16)
+        gh_out[k * 16:(k + 1) * 16, :] = half_sums[k].astype(BF16)
 
     sent(FE.at[:, 1:3], es)
     sent(G.at[0:1, 0:4], ns)
@@ -374,6 +378,17 @@
                 at = TAP_ROW[tx, ty] + tz * 8
                 row, lane = at // 128 * 4, at % 128
                 tg_out[(tx * 3 + ty) * 3 + tz] = v3[row:row + 4, lane:lane + 8]
+
+
+def finish(half_ref, taps_ref, half_out, taps_out, sem):
+    copies = [
+        pltpu.make_async_copy(half_ref, half_out, sem.at[0]),
+        pltpu.make_async_copy(taps_ref, taps_out, sem.at[1]),
+    ]
+    for copy in copies:
+        copy.start()
+    for copy in copies:
+        copy.wait()
 
 
 def body(grad_out, feat_full, filters_full, upsample_weight, filters_half):
@@ -416,10 +431,21 @@
             D((7,)),
             D, D, D, D, D, D, D, D, D, D, D, D,
             D((3,)), D((3,)), D((3,)), D((3,)),
-            D, D, D, D, D, D, pltpu.SemaphoreType.REGULAR,
+            D, D((2,)), D, D((2,)), D, D, pltpu.SemaphoreType.REGULAR,
         ],
         compiler_params=pltpu.CompilerParams(collective_id=0, has_side_effects=True),
     )(grad_out, feat_full, filters_full, upsample_weight, turned)
+    grad_half, taps = pl.pallas_call(
+        finish,
+        out_shape=(
+            jax.ShapeDtypeStruct((32, wide), BF16),
+            jax.ShapeDtypeStruct((27, 4, 8), F32),
+        ),
+        in_specs=[vmem, vmem],
+        out_specs=(anyspace, anyspace),
+        scratch_shapes=[D((2,))],
+        compiler_params=pltpu.CompilerParams(vmem_limit_bytes=1 << 20),
+    )(grad_half, taps)
     return grad_half.reshape(1, 4, 8, wide), taps.reshape(3, 3, 3, 4, 8)
 
 

time: 37.5 us -> 36.6 us (0.976)
  local copies, waits for them, and re-layouts: 1.24 us -> 0 us
    unnamed x2 -> x0, local copies, waits for them, and re-layouts: 1.24 us -> none
    pallas_call x0 -> x1, Pallas kernels: none -> 0.65 us  [body(): pl.pallas_call(finish, out_shape=(jax.ShapeDtypeStruct((32, wide), BF16),...]
where the time goes in v9:
time: 36.6 us; the launch traced here: 36.5 us
  Pallas kernels  35.8 us (98%)
  between operations  0.64 us (2%)
    pallas_call x1, Pallas kernels, body(): pl.pallas_call(kernel, out_shape=(pltpu.VMEM((32, wide), BF16), pltpu.VME...  35.2 us

profile of v9, /device:TPU:1, one launch (start us, length us, event | category | flops | bytes accessed | tf_op | source)
XLA Modules:
  0.0 36.5 jit_solution(1618995576638931960)
XLA Ops:
  0.6 35.2 %shard_map.68 = (bf16[32,512]{1,0:T(8,128)(2,1)S(1)}, f32[27,4,8]{2,1,0:T(4,128)S(1)}) custom-call(bf16[8,2,16,128]{3,2,1,0:T(8,128)(2,1)} %go.1, bf16[8,2,16,128]{3,2,1,0:T(8,128)(2,1)} %fe.1, bf16[3,3,3,128,128]{4,3,2,1,0:T(8,128)(2,1)} %wf.1, bf16[2,2,2,512,128]{4,3,2,1,0:T(8,128)(2,1)} %uw.1, bf16[3,3,3,32,512]{4,3,2,1,0:T(8,128)(2,1)} %bitcast.3), custom_call_target="tpu_custom_call" | custom-call | tf_op jit(solution)/shard_map/pallas_call | solution.py:403
  35.8 0.7 %shard_map.69 = (bf16[32,512]{1,0:T(8,128)(2,1)}, f32[27,4,8]{2,1,0:T(4,128)}) custom-call(bf16[32,512]{1,0:T(8,128)(2,1)S(1)} %get-tuple-element.6.half_ref, f32[27,4,8]{2,1,0:T(4,128)S(1)} %get-tuple-element.7.taps_ref), custom_call_target="tpu_custom_call" | custom-call | tf_op jit(solution)/shard_map/pallas_call | solution.py:438
